TPU v7x, 32 devices: a whole 2x2x4 slice. The times are simulated.
32 devices in a mesh: pa: 4 (over y, core), pb: 8 (over z, x).
Axes of the slice: x: 2, y: 2, z: 4, core: 2. Of those that a mesh axis runs over, the one named last changes fastest.
Arguments:
- excitons: bfloat16 [2, 512, 1024], P(None, 'pa', 'pb'), may hold values from -6 to 6
- screened: bfloat16 [16384, 16384], P('pa', 'pb'), may hold values from -0.25 to 0.25
- phi_val: bfloat16 [16384, 512], P('pa'), may hold values from -0.25 to 0.25
- phi_con: bfloat16 [16384, 1024], P('pb'), may hold values from -0.1875 to 0.1875
Outputs:
- kernel_out: bfloat16 [2, 512, 1024], P(None, 'pa', 'pb')
All inputs are finite; a program needn't handle non-finite values.
Results may differ from a plain program's by a relative error of at most 0.0057.
Values may be sent and summed in bfloat16 or wider, within the bound.
No kernel may reach another device: no remote copies, remote signals or barrier semaphores. Data moves between devices by JAX's collectives and lax.ppermute only.
A program may use at most 192 MiB of HBM per device.

v0:
```python
import jax
import jax.numpy as jnp
from jax import lax
from jax.sharding import PartitionSpec as P


def local(excitons, screened, phi_val, phi_con):
    high = lax.Precision.HIGHEST
    val_rows = lax.all_gather(excitons, "pb", axis=2, tiled=True)
    half_exp = jnp.einsum(
        "evc,qc->evq",
        lax.all_gather(val_rows, "pa", axis=1, tiled=True),
        phi_con,
        preferred_element_type=jnp.float32,
    ).astype(jnp.bfloat16)
    expanded = jnp.einsum("pv,evq->epq", phi_val, half_exp, preferred_element_type=jnp.float32)
    weighted = (screened.astype(jnp.float32)[None] * expanded).astype(jnp.bfloat16)
    partial_value = jnp.einsum("pv,epq->evq", phi_val, weighted, preferred_element_type=jnp.float32)
    con_float = phi_con.astype(jnp.float32)
    terms = jnp.einsum("evq,qc->evc", partial_value, con_float, precision=high)
    columns = lax.psum_scatter(terms, "pb", scatter_dimension=2, tiled=True)
    result = lax.psum_scatter(columns, "pa", scatter_dimension=1, tiled=True)
    return result.astype(jnp.bfloat16)


def solution(mesh):
    placed = (P(None, "pa", "pb"), P("pa", "pb"), P("pa", None), P("pb", None))
    return jax.shard_map(
        local, mesh=mesh, in_specs=placed, out_specs=P(None, "pa", "pb"), check_vma=False
    )
```

profile of v0, /device:TPU:0, one launch (start us, length us, event | category | flops | bytes accessed | tf_op | source)
XLA Modules:
  0.0 260.3 jit_solution(2940196024953835160)
XLA Ops:
  6.5 0.0 all-gather.2.cloned.1.call-start
  6.5 31.1 %all_gather.6 = bf16[2,128,1024]{2,1,0:T(8,128)(2,1)} all-gather(bf16[2,128,128]{2,1,0:T(8,128)(2,1)} %param.4), channel_id=1, replica_groups=mesh['pa'=4,'pb'=8] {'pb'}, dimensions={2}, use_global_device_ids=true | all-gather | bytes 589824 | tf_op jit(solution)/shard_map/all_gather | solution.py:9
  37.6 0.0 all-gather.2.cloned.1.call-update
  37.6 0.0 reduce-scatter.3.cloned.1.call-start
  37.7 18.8 %convert_element_type.13 = f32[4096,2048]{1,0:T(8,128)} convert(bf16[4096,2048]{1,0:T(8,128)(2,1)} %param.5) | non-fusion elementwise | flops 8388608 | bytes 50331648 | tf_op jit(solution)/shard_map/convert_element_type | solution.py:17
  56.5 2.3 all-gather.2.cloned.1.call-done
  58.8 9.3 %fusion.11 = bf16[2,512,2048]{2,1,0:T(8,128)(2,1)} fusion(bf16[2,512,1024]{2,1,0:T(8,128)(2,1)} %all-gather.2.cloned.1.call-done, bf16[2048,1024]{1,0:T(8,128)(2,1)} %param.7), kind=kOutput, calls=%fused_computation.9 | convolution fusion | flops 4294967296 | bytes 10485760 | tf_op jit(solution)/shard_map/evc,qc->evq/dot_general | solution.py:10
  68.1 33.7 %fusion.26 = bf16[2,4096,2048]{2,1,0:T(8,128)(2,1)} fusion(f32[4096,2048]{1,0:T(8,128)} %convert_element_type.13, bf16[4096,512]{1,0:T(8,128)(2,1)} %param.6, bf16[2,512,2048]{2,1,0:T(8,128)(2,1)} %fusion.11), kind=kOutput, calls=%fused_computation.1.clone.clone.1 | convolution fusion | flops 17213423616 | bytes 75497472 | tf_op jit(solution)/shard_map/pv,evq->epq/dot_general | solution.py:16
  101.8 0.0 copy-start
  101.8 22.9 %fusion.1 = f32[2,2048,512]{1,2,0:T(8,128)S(1)} fusion(bf16[4096,512]{1,0:T(8,128)(2,1)} %param.6, bf16[2,4096,2048]{2,1,0:T(8,128)(2,1)} %fusion.26), kind=kOutput, calls=%fused_computation.2 | convolution fusion | flops 17179869184 | bytes 46137344 | tf_op jit(solution)/shard_map/pv,epq->evq/dot_general | solution.py:18
  124.7 0.0 copy-done
  124.7 14.9 %fusion.4 = f32[2,512,1024]{2,1,0:T(8,128)} fusion(f32[2,2048,512]{1,2,0:T(8,128)S(1)} %fusion.1, bf16[2048,1024]{1,0:T(8,128)(2,1)S(1)} %copy-done), kind=kOutput, calls=%fused_computation.4 | convolution fusion | flops 25769803776 | bytes 16777216 | tf_op jit(solution)/shard_map/evq,qc->evc/dot_general | solution.py:20
  139.6 0.0 reduce-scatter.3.cloned.1.call-update
  139.6 0.0 reduce-scatter.5.cloned.1.call-start
  139.6 88.8 %reduce-scatter.3.cloned.1.call-done = f32[2,512,128]{2,1,0:T(8,128)} async-done(((f32[2,512,1024]{2,1,0:T(8,128)}), f32[2,512,128]{2,1,0:T(8,128)}) %reduce-scatter.3.cloned.1.call-update) | async-done | bytes 524304 | tf_op jit(solution)/shard_map/reduce_scatter | solution.py:21
  228.4 0.0 reduce-scatter.5.cloned.1.call-update
  228.4 23.8 %reduce-scatter.5.cloned.1.call-done = f32[2,128,128]{2,1,0:T(8,128)} async-done(((f32[2,512,128]{2,1,0:T(8,128)}), f32[2,128,128]{2,1,0:T(8,128)}) %reduce-scatter.5.cloned.1.call-update) | async-done | bytes 131088 | tf_op jit(solution)/shard_map/reduce_scatter | solution.py:22
  252.3 1.5 convert_element_type.16
Async XLA Ops:
  6.5 52.3 %all-gather.2.cloned.1.call-start = ((), (), s32[]{:S(2)}) async-start(), calls=%async_computation.2 | async-start | bytes 2621440 | tf_op jit(solution)/shard_map/all_gather | solution.py:12
  37.6 190.8 %reduce-scatter.3.cloned.1.call-start = ((), (), s32[]{:S(2)}) async-start(), calls=%async_computation.3 | async-start | bytes 4718592 | tf_op jit(solution)/shard_map/reduce_scatter | solution.py:21
  101.8 22.9 %copy-start = (bf16[2048,1024]{1,0:T(8,128)(2,1)S(1)}, bf16[2048,1024]{1,0:T(8,128)(2,1)}, u32[]{:S(2)}) copy-start(bf16[2048,1024]{1,0:T(8,128)(2,1)} %param.7) | copy-start | bytes 12582916
  139.6 112.7 %reduce-scatter.5.cloned.1.call-start = ((), (), s32[]{:S(2)}) async-start(), calls=%async_computation.4 | async-start | bytes 655360 | tf_op jit(solution)/shard_map/reduce_scatter | solution.py:22
Sparse Core Ops, SparseCore 0:
  37.8 20.9 all-gather.1
  139.7 88.6 reduce-scatter.2
  230.9 21.3 reduce-scatter.4
where the time goes:
time: 261 us; the launch traced here: 260 us
  waiting for transfers between devices  115 us (44%)
  matrix products  80.8 us (31%)
  blocking collectives  31.1 us (12%)
  other arithmetic  20.4 us (8%)
  between operations  13.1 us (5%)
    reduce_scatter x1, waiting for transfers between devices, local(): columns = lax.psum_scatter(terms, 'pb', scatter_dimension=2, tiled=True)  88.8 us
    dot_general x1, matrix products, local(): jnp.einsum('pv,evq->epq', phi_val, half_exp, preferred_element_type=jnp.f...  33.7 us
    all_gather x1, blocking collectives, local(): val_rows = lax.all_gather(excitons, 'pb', axis=2, tiled=True)  31.1 us
    reduce_scatter x1, waiting for transfers between devices, local(): result = lax.psum_scatter(columns, 'pa', scatter_dimension=1, tiled=True)  23.8 us
    dot_general x1, matrix products, local(): jnp.einsum('pv,epq->evq', phi_val, weighted, preferred_element_type=jnp.f...  22.9 us
    convert_element_type x1, other arithmetic, local(): screened.astype(jnp.float32)[None] * expanded  18.8 us
    dot_general x1, matrix products, local(): terms = jnp.einsum('evq,qc->evc', partial_value, con_float, precision=high)  14.9 us
    dot_general x1, matrix products, local(): jnp.einsum('evc,qc->evq', lax.all_gather(val_rows, 'pa', axis=1, tiled=Tr...  9.34 us
  transfers between devices with their start and end apart: 3, of which 3 were waited for; matrix products, arithmetic and copies ran while one was open for 7% of the time, Pallas kernels for 0%

commit v1 on v0

v1 whole, which is shorter than its diff:
```python
import functools

import jax
import jax.numpy as jnp
from jax import lax
from jax.experimental import pallas as pl
from jax.experimental.pallas import tpu as pltpu
from jax.sharding import PartitionSpec as P

TILE_P = 512
LANES = 128


def xor_pairs(size, mask):
    return [(i, i ^ mask) for i in range(size)]


def xor_columns(value, me, width):
    columns = value.shape[1]
    bit = 1
    while bit * width < columns:
        half = bit * width
        flipped = jnp.concatenate(
            [value[:, (k ^ 1) * half : ((k ^ 1) + 1) * half] for k in range(columns // half)], axis=1
        )
        value = jnp.where(lax.broadcast((me & bit) != 0, value.shape), flipped, value)
        bit *= 2
    return value


def fused_kernel(order_a, order_b, rows_keep, me_ref, *refs):
    count = len(order_a)
    exc_refs = refs[:count]
    con_ref, val_ref, scr_ref = refs[count : count + 3]
    keep_refs = refs[count + 3 : count + 3 + rows_keep]
    send_ref = refs[count + 3 + rows_keep]
    exc, half, acc, terms = refs[count + 4 + rows_keep :]
    vb, nc = exc_refs[0].shape
    cb = nc // len(order_b)
    step = pl.program_id(0)
    me_a, me_b = me_ref[0], me_ref[1]
    aligned = cb % LANES == 0

    def row(rel):
        return pl.ds(pl.multiple_of((me_a ^ rel) * vb, vb), vb)

    def column(rel):
        return pl.ds(pl.multiple_of((me_b ^ rel) * cb, cb), cb)

    @pl.when(step == 0)
    def _():
        for i, rel_a in enumerate(order_a):
            if aligned:
                for j, rel_b in enumerate(order_b):
                    exc[row(rel_a), column(rel_b)] = exc_refs[i][:, j * cb : (j + 1) * cb]
            else:
                place = {rel_b: j for j, rel_b in enumerate(order_b)}
                value = exc_refs[i][...]
                value = jnp.concatenate(
                    [value[:, place[k] * cb : (place[k] + 1) * cb] for k in range(len(order_b))], axis=1
                )
                exc[row(rel_a), :] = xor_columns(value, me_b, cb)
        half[...] = lax.dot_general(
            exc[...], con_ref[...], (((1,), (1,)), ((), ())), preferred_element_type=jnp.float32
        ).astype(half.dtype)
        acc[...] = jnp.zeros_like(acc)

    val = val_ref[...]
    expanded = jnp.dot(val, half[...], preferred_element_type=jnp.float32)
    weighted = (scr_ref[...].astype(jnp.float32) * expanded).astype(jnp.bfloat16)
    acc[...] += lax.dot_general(
        val, weighted, (((0,), (0,)), ((), ())), preferred_element_type=jnp.float32
    )

    @pl.when(step == pl.num_programs(0) - 1)
    def _():
        terms[...] = jnp.dot(
            acc[...].astype(jnp.bfloat16), con_ref[...], preferred_element_type=jnp.float32
        )
        for i, rel_a in enumerate(order_a):
            if i < rows_keep:
                target, rows = keep_refs[i], slice(0, vb)
            else:
                target, rows = send_ref, slice((i - rows_keep) * vb, (i - rows_keep + 1) * vb)
            if aligned:
                for j, rel_b in enumerate(order_b):
                    target[rows, j * cb : (j + 1) * cb] = terms[row(rel_a), column(rel_b)].astype(target.dtype)
            else:
                value = xor_columns(terms[row(rel_a), :], me_b, cb)
                target[rows, :] = jnp.concatenate(
                    [value[:, k * cb : (k + 1) * cb] for k in order_b], axis=1
                ).astype(target.dtype)


def apply_block(me, exc_rows, con, val, screened, order_a, order_b):
    count = len(exc_rows)
    vb, nc = exc_rows[0].shape
    nv = count * vb
    np_, nq = screened.shape
    tile = min(TILE_P, np_)
    keep = max(count // 2, 1)
    whole = lambda shape: pl.BlockSpec(shape, lambda i, m: (0, 0), pipeline_mode=pl.Buffered(1))
    flops = 2 * nv * nc * nq * 2 + 4 * np_ * nq * nv
    *kept, send = pl.pallas_call(
        functools.partial(fused_kernel, order_a, order_b, keep),
        out_shape=[jax.ShapeDtypeStruct((vb, nc), jnp.float32)] * keep
        + [jax.ShapeDtypeStruct((nv - keep * vb, nc), jnp.bfloat16)],
        grid_spec=pltpu.PrefetchScalarGridSpec(
            num_scalar_prefetch=1,
            grid=(np_ // tile,),
            in_specs=[whole((vb, nc))] * count
            + [
                whole((nq, nc)),
                pl.BlockSpec((tile, nv), lambda i, m: (i, 0)),
                pl.BlockSpec((tile, nq), lambda i, m: (i, 0)),
            ],
            out_specs=[whole((vb, nc))] * keep + [whole((nv - keep * vb, nc))],
            scratch_shapes=[
                pltpu.VMEM((nv, nc), jnp.bfloat16),
                pltpu.VMEM((nv, nq), jnp.bfloat16),
                pltpu.VMEM((nv, nq), jnp.float32),
                pltpu.VMEM((nv, nc), jnp.float32),
            ],
        ),
        cost_estimate=pl.CostEstimate(
            flops=flops, transcendentals=0, bytes_accessed=2 * (np_ * nq + np_ * nv + nq * nc)
        ),
    )(me, *exc_rows, con, val, screened)
    return kept, send


def solution(mesh):
    na, nb = mesh.shape["pa"], mesh.shape["pb"]
    low_a, high_a = 2, na // 2
    high_b = min(nb, 4)
    low_b = nb // high_b
    order_a = [h * low_a + l for l in range(low_a) for h in range(high_a)]
    order_b = [h * low_b + l for l in range(low_b) for h in range(high_b)]

    def to_a(x, mask):
        return lax.ppermute(x, "pa", xor_pairs(na, mask))

    def to_b(x, mask):
        return lax.ppermute(x, "pb", xor_pairs(nb, mask))

    def local(excitons, screened, phi_val, phi_con):
        me = jnp.stack([lax.axis_index("pa"), lax.axis_index("pb")]).astype(jnp.int32)
        count = excitons.shape[0]
        vb, cb = excitons.shape[1:]
        f32, bf16 = jnp.float32, jnp.bfloat16
        wide = high_b * cb

        def gather(e):
            own = excitons[e]
            line = jnp.concatenate([own] + [to_b(own, k * low_b) for k in range(1, high_b)], 1)
            row = jnp.concatenate([line] + [to_b(line, k) for k in range(1, low_b)], 1)
            rows = [row] + [to_a(row, k * low_a) for k in range(1, high_a)]
            return rows + [to_a(r, k) for k in range(1, low_a) for r in rows]

        def scatter(kept, send):
            other = to_a(send, 1)
            rows = [k + other[i * vb : (i + 1) * vb].astype(f32) for i, k in enumerate(kept)]
            out = rows[0]
            for k in range(1, high_a):
                out = out + to_a(rows[k].astype(bf16), k * low_a).astype(f32)
            total = out[:, :wide]
            for k in range(1, low_b):
                total = total + to_b(out[:, k * wide : (k + 1) * wide].astype(bf16), k).astype(f32)
            return total

        totals = []
        for e in range(count):
            kept, send = apply_block(me, gather(e), phi_con, phi_val, screened, order_a, order_b)
            totals.append(scatter(kept, send))
        both = jnp.stack(totals)
        result = both[:, :, :cb]
        for k in range(1, high_b):
            result = result + to_b(both[:, :, k * cb : (k + 1) * cb].astype(bf16), k * low_b).astype(f32)
        return result.astype(bf16)

    placed = (P(None, "pa", "pb"), P("pa", "pb"), P("pa", None), P("pb", None))
    return jax.shard_map(
        local, mesh=mesh, in_specs=placed, out_specs=P(None, "pa", "pb"), check_vma=False
    )
```

time: 261 us -> 122 us (0.47)
  waiting for transfers between devices: 115 us -> 27 us
  matrix products: 80.8 us -> 0 us
  Pallas kernels: 0 us -> 59.4 us
  blocking collectives: 31.1 us -> 0 us
  starting transfers between devices: 0.09 us -> 27.5 us
  other arithmetic: 20.4 us -> 2.79 us
  between operations: 13.1 us -> 0.26 us
  local copies, waits for them, and re-layouts: 0.01 us -> 4.61 us
    reduce_scatter x2 -> x0, waiting for transfers between devices: 113 us -> none  [the longest x1 88.8 us: local(): columns = lax.psum_scatter(terms, 'pb', scatter_dimension=2, tiled=True)]
    dot_general x4 -> x0, matrix products: 80.8 us -> none  [the longest x1 33.7 us: local(): jnp.einsum('pv,evq->epq', phi_val, half_exp, preferred_element_type=jnp.f...]
    pallas_call x0 -> x2, Pallas kernels: none -> 59.4 us  [apply_block(): pl.pallas_call(functools.partial(fused_kernel, order_a, order_b, keep), o...]
    all_gather x1 -> x0, blocking collectives: 31.1 us -> none  [local(): val_rows = lax.all_gather(excitons, 'pb', axis=2, tiled=True)]
    ppermute x0 -> x23, starting transfers between devices: none -> 27.5 us  [the longest x13 20.1 us: to_b(): return lax.ppermute(x, 'pb', xor_pairs(nb, mask))]
    ppermute x0 -> x23, waiting for transfers between devices: none -> 27 us  [the longest x10 13.5 us: to_a(): return lax.ppermute(x, 'pa', xor_pairs(na, mask))]
    convert_element_type x2 -> x3, other arithmetic: 20.4 us -> 1.82 us  [the longest x2 1.16 us: scatter(): out = out + to_a(rows[k].astype(bf16), k * low_a).astype(f32)]
    unnamed x2 -> x29, local copies, waits for them, and re-layouts: 0.01 us -> 3.73 us
  transfers between devices with their start and end apart: 3 -> 23, of which waited for: 3 -> 11; matrix products, arithmetic and copies ran while one was open for 7% -> 2% of each run, Pallas kernels for 0% -> 49%
where the time goes in v1:
time: 122 us
  Pallas kernels  59.4 us (49%)
  starting transfers between devices  27.5 us (23%)
  waiting for transfers between devices  27 us (22%)
  local copies, waits for them, and re-layouts  4.61 us (4%)
  other arithmetic  2.79 us (2%)
    pallas_call x2, Pallas kernels, apply_block(): pl.pallas_call(functools.partial(fused_kernel, order_a, order_b, keep), o...  59.4 us
    ppermute x13, starting transfers between devices, to_b(): return lax.ppermute(x, 'pb', xor_pairs(nb, mask))  20.1 us
    ppermute x10, waiting for transfers between devices, to_a(): return lax.ppermute(x, 'pa', xor_pairs(na, mask))  13.5 us
    ppermute x13, waiting for transfers between devices, to_b(): return lax.ppermute(x, 'pb', xor_pairs(nb, mask))  13.4 us
    ppermute x10, starting transfers between devices, to_a(): return lax.ppermute(x, 'pa', xor_pairs(na, mask))  7.4 us
    unnamed x29, local copies, waits for them, and re-layouts  3.73 us
  transfers between devices with their start and end apart: 23, of which 11 were waited for; matrix products, arithmetic and copies ran while one was open for 2% of the time, Pallas kernels for 49%

profile of v1, /device:TPU:0, one launch (start us, length us, event | category | flops | bytes accessed | tf_op | source)
XLA Modules:
  0.0 121.5 jit_solution(2134284578026158439)
XLA Ops:
  0.8 3.1 %collective-permute-start.10 = (bf16[128,128]{1,0:T(8,128)(2,1)S(1)}, bf16[128,128]{1,0:T(8,128)(2,1)S(1)}, u32[]{:S(2)}, u32[]{:S(2)}) collective-permute-start(bf16[128,128]{1,0:T(8,128)(2,1)S(1)} %get-tuple-element.20), channel_id=1, source_target_pairs={{0,2},{1,3},{2,0},{3,1},{4,6},{5,7},{6,4},{7,5},{8,10},{9,11},{10,... | collective-permute-start | bytes 98312 | tf_op jit(solution)/shard_map/ppermute | solution.py:144
  3.8 2.6 %collective-permute-start.11 = (bf16[128,128]{1,0:T(8,128)(2,1)S(1)}, bf16[128,128]{1,0:T(8,128)(2,1)S(1)}, u32[]{:S(2)}, u32[]{:S(2)}) collective-permute-start(bf16[128,128]{1,0:T(8,128)(2,1)S(1)} %get-tuple-element.20), channel_id=1, source_target_pairs={{0,4},{1,5},{2,6},{3,7},{4,0},{5,1},{6,2},{7,3},{8,12},{9,13},{10,... | collective-permute-start | bytes 98312 | tf_op jit(solution)/shard_map/ppermute | solution.py:144
  7.3 3.5 %collective-permute-start.1 = (bf16[128,128]{1,0:T(8,128)(2,1)S(1)}, bf16[128,128]{1,0:T(8,128)(2,1)S(1)}, u32[]{:S(2)}, u32[]{:S(2)}) collective-permute-start(bf16[128,128]{1,0:T(8,128)(2,1)S(1)} %get-tuple-element.21), channel_id=1, source_target_pairs={{0,4},{1,5},{2,6},{3,7},{4,0},{5,1},{6,2},{7,3},{8,12},{9,13},{10,... | collective-permute-start | bytes 98312 | tf_op jit(solution)/shard_map/ppermute | solution.py:144
  12.2 1.6 %collective-permute-start.13 = (bf16[128,512]{1,0:T(8,128)(2,1)S(1)}, bf16[128,512]{1,0:T(8,128)(2,1)S(1)}, u32[]{:S(2)}, u32[]{:S(2)}) collective-permute-start(bf16[128,512]{1,0:T(8,128)(2,1)S(1)} %pad_maximum_fusion.2), channel_id=1, source_target_pairs={{0,1},{1,0},{2,3},{3,2},{4,5},{5,4},{6,7},{7,6},{8,9},{9,8},{10,11... | collective-permute-start | bytes 393224 | tf_op jit(solution)/shard_map/ppermute | solution.py:144
  13.7 3.7 %collective-permute-done.2 = bf16[128,128]{1,0:T(8,128)(2,1)S(1)} collective-permute-done((bf16[128,128]{1,0:T(8,128)(2,1)S(1)}, bf16[128,128]{1,0:T(8,128)(2,1)S(1)}, u32[]{:S(2)}, u32[]{:S(2)}) %collective-permute-start.2) | collective-permute-done | bytes 32800 | tf_op jit(solution)/shard_map/ppermute | solution.py:144
  17.4 1.6 %collective-permute-start.3 = (bf16[128,512]{1,0:T(8,128)(2,1)S(1)}, bf16[128,512]{1,0:T(8,128)(2,1)S(1)}, u32[]{:S(2)}, u32[]{:S(2)}) collective-permute-start(bf16[128,512]{1,0:T(8,128)(2,1)S(1)} %pad_maximum_fusion.1), channel_id=1, source_target_pairs={{0,1},{1,0},{2,3},{3,2},{4,5},{5,4},{6,7},{7,6},{8,9},{9,8},{10,11... | collective-permute-start | bytes 393224 | tf_op jit(solution)/shard_map/ppermute | solution.py:144
  19.1 1.6 %collective-permute-start.14 = (bf16[128,1024]{1,0:T(8,128)(2,1)S(1)}, bf16[128,1024]{1,0:T(8,128)(2,1)S(1)}, u32[]{:S(2)}, u32[]{:S(2)}) collective-permute-start(bf16[128,1024]{1,0:T(8,128)(2,1)S(1)} %constant_dynamic-update-slice_fusion.5.refs_0_), channel_id=1, source_target_pairs={{0,16},{8,24},{16,0},{24,8},{1,17},{9,25},{17,1},{25,9},{2,18},{10... | collective-permute-start | bytes 786440 | tf_op jit(solution)/shard_map/ppermute | solution.py:141
  20.7 1.8 %collective-permute-done.3 = bf16[128,512]{1,0:T(8,128)(2,1)S(1)} collective-permute-done((bf16[128,512]{1,0:T(8,128)(2,1)S(1)}, bf16[128,512]{1,0:T(8,128)(2,1)S(1)}, u32[]{:S(2)}, u32[]{:S(2)}) %collective-permute-start.3) | collective-permute-done | bytes 131104 | tf_op jit(solution)/shard_map/ppermute | solution.py:144
  22.5 1.6 %collective-permute-start.4 = (bf16[128,1024]{1,0:T(8,128)(2,1)S(1)}, bf16[128,1024]{1,0:T(8,128)(2,1)S(1)}, u32[]{:S(2)}, u32[]{:S(2)}) collective-permute-start(bf16[128,1024]{1,0:T(8,128)(2,1)S(1)} %constant_dynamic-update-slice_fusion.refs_0_), channel_id=1, source_target_pairs={{0,16},{8,24},{16,0},{24,8},{1,17},{9,25},{17,1},{25,9},{2,18},{10... | collective-permute-start | bytes 786440 | tf_op jit(solution)/shard_map/ppermute | solution.py:141
  24.1 3.1 %collective-permute-done.14.refs_1_ = bf16[128,1024]{1,0:T(8,128)(2,1)S(1)} collective-permute-done((bf16[128,1024]{1,0:T(8,128)(2,1)S(1)}, bf16[128,1024]{1,0:T(8,128)(2,1)S(1)}, u32[]{:S(2)}, u32[]{:S(2)}) %collective-permute-start.14) | collective-permute-done | bytes 262176 | tf_op jit(solution)/shard_map/ppermute | solution.py:141
  28.3 1.6 %collective-permute-done.4.refs_1_ = bf16[128,1024]{1,0:T(8,128)(2,1)S(1)} collective-permute-done((bf16[128,1024]{1,0:T(8,128)(2,1)S(1)}, bf16[128,1024]{1,0:T(8,128)(2,1)S(1)}, u32[]{:S(2)}, u32[]{:S(2)}) %collective-permute-start.4) | collective-permute-done | bytes 262176 | tf_op jit(solution)/shard_map/ppermute | solution.py:141
  31.5 29.7 %shard_map.47 = (f32[128,1024]{1,0:T(8,128)}, f32[128,1024]{1,0:T(8,128)}, bf16[256,1024]{1,0:T(8,128)(2,1)}) custom-call(s32[2]{0:T(128)} %pad_add_fusion.me_ref, bf16[128,1024]{1,0:T(8,128)(2,1)} %copy-done.4, bf16[128,1024]{1,0:T(8,128)(2,1)} %copy-done.6, bf16[128,1024]{1,0:T(8,128)(2,1)} %copy-done.7, bf16[128,1024]{1,0:T(8,128)(2,1)} %copy-done.8, ...), custom_call_target="tpu_custom_call" | custom-call | flops 21474836480 | bytes 25165824 | tf_op jit(solution)/shard_map/pallas_call | solution.py:104
  63.2 29.7 %shard_map.46 = (f32[128,1024]{1,0:T(8,128)}, f32[128,1024]{1,0:T(8,128)}, bf16[256,1024]{1,0:T(8,128)(2,1)}) custom-call(s32[2]{0:T(128)} %pad_add_fusion.me_ref, bf16[128,1024]{1,0:T(8,128)(2,1)} %copy-done.3, bf16[128,1024]{1,0:T(8,128)(2,1)} %copy-done.5, bf16[128,1024]{1,0:T(8,128)(2,1)} %copy-done.9, bf16[128,1024]{1,0:T(8,128)(2,1)} %copy-done.10, ...), custom_call_target="tpu_custom_call" | custom-call | flops 21474836480 | bytes 25165824 | tf_op jit(solution)/shard_map/pallas_call | solution.py:104
  93.0 1.6 %collective-permute-start.18 = (bf16[128,1024]{1,0:T(8,128)(2,1)S(1)}, bf16[128,1024]{1,0:T(8,128)(2,1)S(1)}, u32[]{:S(2)}, u32[]{:S(2)}) collective-permute-start(bf16[128,1024]{1,0:T(8,128)(2,1)S(1)} %add_convert_fusion), channel_id=1, source_target_pairs={{0,16},{8,24},{16,0},{24,8},{1,17},{9,25},{17,1},{25,9},{2,18},{10... | collective-permute-start | bytes 786440 | tf_op jit(solution)/shard_map/ppermute | solution.py:141
  96.1 1.6 %collective-permute-start.8 = (bf16[128,1024]{1,0:T(8,128)(2,1)S(1)}, bf16[128,1024]{1,0:T(8,128)(2,1)S(1)}, u32[]{:S(2)}, u32[]{:S(2)}) collective-permute-start(bf16[128,1024]{1,0:T(8,128)(2,1)S(1)} %add_convert_fusion.1), channel_id=1, source_target_pairs={{0,16},{8,24},{16,0},{24,8},{1,17},{9,25},{17,1},{25,9},{2,18},{10... | collective-permute-start | bytes 786440 | tf_op jit(solution)/shard_map/ppermute | solution.py:141
  97.7 4.5 %collective-permute-done.18 = bf16[128,1024]{1,0:T(8,128)(2,1)S(1)} collective-permute-done((bf16[128,1024]{1,0:T(8,128)(2,1)S(1)}, bf16[128,1024]{1,0:T(8,128)(2,1)S(1)}, u32[]{:S(2)}, u32[]{:S(2)}) %collective-permute-start.18) | collective-permute-done | bytes 262176 | tf_op jit(solution)/shard_map/ppermute | solution.py:141
  102.4 1.2 %collective-permute-start.19 = (bf16[128,512]{1,0:T(8,128)(2,1)S(1)}, bf16[128,512]{1,0:T(8,128)(2,1)S(1)}, u32[]{:S(2)}, u32[]{:S(2)}) collective-permute-start(bf16[128,512]{1,0:T(8,128)(2,1)S(1)} %slice.106), channel_id=1, source_target_pairs={{0,1},{1,0},{2,3},{3,2},{4,5},{5,4},{6,7},{7,6},{8,9},{9,8},{10,11... | collective-permute-start | bytes 393224 | tf_op jit(solution)/shard_map/ppermute | solution.py:144
  103.6 3.8 %collective-permute-done.8 = bf16[128,1024]{1,0:T(8,128)(2,1)S(1)} collective-permute-done((bf16[128,1024]{1,0:T(8,128)(2,1)S(1)}, bf16[128,1024]{1,0:T(8,128)(2,1)S(1)}, u32[]{:S(2)}, u32[]{:S(2)}) %collective-permute-start.8) | collective-permute-done | bytes 262176 | tf_op jit(solution)/shard_map/ppermute | solution.py:141
  107.5 1.2 collective-permute-start.9
  108.7 3.8 %collective-permute-done.9 = bf16[128,512]{1,0:T(8,128)(2,1)S(1)} collective-permute-done((bf16[128,512]{1,0:T(8,128)(2,1)S(1)}, bf16[128,512]{1,0:T(8,128)(2,1)S(1)}, u32[]{:S(2)}, u32[]{:S(2)}) %collective-permute-start.9) | collective-permute-done | bytes 131104 | tf_op jit(solution)/shard_map/ppermute | solution.py:144
  112.8 2.0 %collective-permute-start.21 = (bf16[2,128,128]{2,1,0:T(8,128)(2,1)S(1)}, bf16[2,128,128]{2,1,0:T(8,128)(2,1)S(1)}, u32[]{:S(2)}, u32[]{:S(2)}) collective-permute-start(bf16[2,128,128]{2,1,0:T(8,128)(2,1)S(1)} %get-tuple-element.19), channel_id=1, source_target_pairs={{0,4},{1,5},{2,6},{3,7},{4,0},{5,1},{6,2},{7,3},{8,12},{9,13},{10,... | collective-permute-start | bytes 196616 | tf_op jit(solution)/shard_map/ppermute | solution.py:144
  114.8 2.3 %collective-permute-start.22 = (bf16[2,128,128]{2,1,0:T(8,128)(2,1)S(1)}, bf16[2,128,128]{2,1,0:T(8,128)(2,1)S(1)}, u32[]{:S(2)}, u32[]{:S(2)}) collective-permute-start(bf16[2,128,128]{2,1,0:T(8,128)(2,1)S(1)} %get-tuple-element.18), channel_id=1, source_target_pairs={{0,6},{1,7},{2,4},{3,5},{4,2},{5,3},{6,0},{7,1},{8,14},{9,15},{10,... | collective-permute-start | bytes 196616 | tf_op jit(solution)/shard_map/ppermute | solution.py:144
  117.2 1.6 %collective-permute-done.21 = bf16[2,128,128]{2,1,0:T(8,128)(2,1)S(1)} collective-permute-done((bf16[2,128,128]{2,1,0:T(8,128)(2,1)S(1)}, bf16[2,128,128]{2,1,0:T(8,128)(2,1)S(1)}, u32[]{:S(2)}, u32[]{:S(2)}) %collective-permute-start.21) | collective-permute-done | bytes 65568 | tf_op jit(solution)/shard_map/ppermute | solution.py:144
  118.7 2.2 %collective-permute-done.22 = bf16[2,128,128]{2,1,0:T(8,128)(2,1)S(1)} collective-permute-done((bf16[2,128,128]{2,1,0:T(8,128)(2,1)S(1)}, bf16[2,128,128]{2,1,0:T(8,128)(2,1)S(1)}, u32[]{:S(2)}, u32[]{:S(2)}) %collective-permute-start.22) | collective-permute-done | bytes 65568 | tf_op jit(solution)/shard_map/ppermute | solution.py:144
  (70 shorter events, 10.4 us)
Async XLA Ops:
  0.8 10.8 %collective-permute-start.10 = (bf16[128,128]{1,0:T(8,128)(2,1)S(1)}, bf16[128,128]{1,0:T(8,128)(2,1)S(1)}, u32[]{:S(2)}, u32[]{:S(2)}) collective-permute-start(bf16[128,128]{1,0:T(8,128)(2,1)S(1)} %get-tuple-element.20), channel_id=1, source_target_pairs={{0,2},{1,3},{2,0},{3,1},{4,6},{5,7},{6,4},{7,5},{8,10},{9,11},{10,... | collective-permute-start | bytes 98312 | tf_op jit(solution)/shard_map/ppermute | solution.py:144
  3.8 7.9 %collective-permute-start.11 = (bf16[128,128]{1,0:T(8,128)(2,1)S(1)}, bf16[128,128]{1,0:T(8,128)(2,1)S(1)}, u32[]{:S(2)}, u32[]{:S(2)}) collective-permute-start(bf16[128,128]{1,0:T(8,128)(2,1)S(1)} %get-tuple-element.20), channel_id=1, source_target_pairs={{0,4},{1,5},{2,6},{3,7},{4,0},{5,1},{6,2},{7,3},{8,12},{9,13},{10,... | collective-permute-start | bytes 98312 | tf_op jit(solution)/shard_map/ppermute | solution.py:144
  6.4 5.7 %collective-permute-start.12 = (bf16[128,128]{1,0:T(8,128)(2,1)S(1)}, bf16[128,128]{1,0:T(8,128)(2,1)S(1)}, u32[]{:S(2)}, u32[]{:S(2)}) collective-permute-start(bf16[128,128]{1,0:T(8,128)(2,1)S(1)} %get-tuple-element.20), channel_id=1, source_target_pairs={{0,6},{1,7},{2,4},{3,5},{4,2},{5,3},{6,0},{7,1},{8,14},{9,15},{10,... | collective-permute-start | bytes 98312 | tf_op jit(solution)/shard_map/ppermute | solution.py:144
  6.4 7.3 %collective-permute-start = (bf16[128,128]{1,0:T(8,128)(2,1)S(1)}, bf16[128,128]{1,0:T(8,128)(2,1)S(1)}, u32[]{:S(2)}, u32[]{:S(2)}) collective-permute-start(bf16[128,128]{1,0:T(8,128)(2,1)S(1)} %get-tuple-element.21), channel_id=1, source_target_pairs={{0,2},{1,3},{2,0},{3,1},{4,6},{5,7},{6,4},{7,5},{8,10},{9,11},{10,... | collective-permute-start | bytes 98312 | tf_op jit(solution)/shard_map/ppermute | solution.py:144
  7.3 6.4 %collective-permute-start.1 = (bf16[128,128]{1,0:T(8,128)(2,1)S(1)}, bf16[128,128]{1,0:T(8,128)(2,1)S(1)}, u32[]{:S(2)}, u32[]{:S(2)}) collective-permute-start(bf16[128,128]{1,0:T(8,128)(2,1)S(1)} %get-tuple-element.21), channel_id=1, source_target_pairs={{0,4},{1,5},{2,6},{3,7},{4,0},{5,1},{6,2},{7,3},{8,12},{9,13},{10,... | collective-permute-start | bytes 98312 | tf_op jit(solution)/shard_map/ppermute | solution.py:144
  11.6 5.8 %collective-permute-start.2 = (bf16[128,128]{1,0:T(8,128)(2,1)S(1)}, bf16[128,128]{1,0:T(8,128)(2,1)S(1)}, u32[]{:S(2)}, u32[]{:S(2)}) collective-permute-start(bf16[128,128]{1,0:T(8,128)(2,1)S(1)} %get-tuple-element.21), channel_id=1, source_target_pairs={{0,6},{1,7},{2,4},{3,5},{4,2},{5,3},{6,0},{7,1},{8,14},{9,15},{10,... | collective-permute-start | bytes 98312 | tf_op jit(solution)/shard_map/ppermute | solution.py:144
  12.2 6.9 %collective-permute-start.13 = (bf16[128,512]{1,0:T(8,128)(2,1)S(1)}, bf16[128,512]{1,0:T(8,128)(2,1)S(1)}, u32[]{:S(2)}, u32[]{:S(2)}) collective-permute-start(bf16[128,512]{1,0:T(8,128)(2,1)S(1)} %pad_maximum_fusion.2), channel_id=1, source_target_pairs={{0,1},{1,0},{2,3},{3,2},{4,5},{5,4},{6,7},{7,6},{8,9},{9,8},{10,11... | collective-permute-start | bytes 393224 | tf_op jit(solution)/shard_map/ppermute | solution.py:144
  17.4 5.0 %collective-permute-start.3 = (bf16[128,512]{1,0:T(8,128)(2,1)S(1)}, bf16[128,512]{1,0:T(8,128)(2,1)S(1)}, u32[]{:S(2)}, u32[]{:S(2)}) collective-permute-start(bf16[128,512]{1,0:T(8,128)(2,1)S(1)} %pad_maximum_fusion.1), channel_id=1, source_target_pairs={{0,1},{1,0},{2,3},{3,2},{4,5},{5,4},{6,7},{7,6},{8,9},{9,8},{10,11... | collective-permute-start | bytes 393224 | tf_op jit(solution)/shard_map/ppermute | solution.py:144
  19.1 8.1 %collective-permute-start.14 = (bf16[128,1024]{1,0:T(8,128)(2,1)S(1)}, bf16[128,1024]{1,0:T(8,128)(2,1)S(1)}, u32[]{:S(2)}, u32[]{:S(2)}) collective-permute-start(bf16[128,1024]{1,0:T(8,128)(2,1)S(1)} %constant_dynamic-update-slice_fusion.5.refs_0_), channel_id=1, source_target_pairs={{0,16},{8,24},{16,0},{24,8},{1,17},{9,25},{17,1},{25,9},{2,18},{10... | collective-permute-start | bytes 786440 | tf_op jit(solution)/shard_map/ppermute | solution.py:141
  22.5 7.5 %collective-permute-start.4 = (bf16[128,1024]{1,0:T(8,128)(2,1)S(1)}, bf16[128,1024]{1,0:T(8,128)(2,1)S(1)}, u32[]{:S(2)}, u32[]{:S(2)}) collective-permute-start(bf16[128,1024]{1,0:T(8,128)(2,1)S(1)} %constant_dynamic-update-slice_fusion.refs_0_), channel_id=1, source_target_pairs={{0,16},{8,24},{16,0},{24,8},{1,17},{9,25},{17,1},{25,9},{2,18},{10... | collective-permute-start | bytes 786440 | tf_op jit(solution)/shard_map/ppermute | solution.py:141
  24.1 5.9 %collective-permute-start.15 = (bf16[128,1024]{1,0:T(8,128)(2,1)S(1)}, bf16[128,1024]{1,0:T(8,128)(2,1)S(1)}, u32[]{:S(2)}, u32[]{:S(2)}) collective-permute-start(bf16[128,1024]{1,0:T(8,128)(2,1)S(1)} %constant_dynamic-update-slice_fusion.5.refs_0_), channel_id=1, source_target_pairs={{0,8},{8,0},{16,24},{24,16},{1,9},{9,1},{17,25},{25,17},{2,10},{10... | collective-permute-start | bytes 786440 | tf_op jit(solution)/shard_map/ppermute | solution.py:141
  27.2 2.8 %collective-permute-start.16 = (bf16[128,1024]{1,0:T(8,128)(2,1)S(1)}, bf16[128,1024]{1,0:T(8,128)(2,1)S(1)}, u32[]{:S(2)}, u32[]{:S(2)}) collective-permute-start(bf16[128,1024]{1,0:T(8,128)(2,1)S(1)} %collective-permute-done.14.refs_1_), channel_id=1, source_target_pairs={{0,8},{8,0},{16,24},{24,16},{1,9},{9,1},{17,25},{25,17},{2,10},{10... | collective-permute-start | bytes 786440 | tf_op jit(solution)/shard_map/ppermute | solution.py:141
  27.8 33.9 %collective-permute-start.5 = (bf16[128,1024]{1,0:T(8,128)(2,1)S(1)}, bf16[128,1024]{1,0:T(8,128)(2,1)S(1)}, u32[]{:S(2)}, u32[]{:S(2)}) collective-permute-start(bf16[128,1024]{1,0:T(8,128)(2,1)S(1)} %constant_dynamic-update-slice_fusion.refs_0_), channel_id=1, source_target_pairs={{0,8},{8,0},{16,24},{24,16},{1,9},{9,1},{17,25},{25,17},{2,10},{10... | collective-permute-start | bytes 786440 | tf_op jit(solution)/shard_map/ppermute | solution.py:141
  30.0 31.8 %collective-permute-start.6 = (bf16[128,1024]{1,0:T(8,128)(2,1)S(1)}, bf16[128,1024]{1,0:T(8,128)(2,1)S(1)}, u32[]{:S(2)}, u32[]{:S(2)}) collective-permute-start(bf16[128,1024]{1,0:T(8,128)(2,1)S(1)} %collective-permute-done.4.refs_1_), channel_id=1, source_target_pairs={{0,8},{8,0},{16,24},{24,16},{1,9},{9,1},{17,25},{25,17},{2,10},{10... | collective-permute-start | bytes 786440 | tf_op jit(solution)/shard_map/ppermute | solution.py:141
  61.2 41.0 %copy-start = (f32[128,1024]{1,0:T(8,128)S(1)}, f32[128,1024]{1,0:T(8,128)}, u32[]{:S(2)}) copy-start(f32[128,1024]{1,0:T(8,128)} %get-tuple-element.14) | copy-start | bytes 1572868
  61.2 31.7 %collective-permute-start.17 = (bf16[256,1024]{1,0:T(8,128)(2,1)}, bf16[256,1024]{1,0:T(8,128)(2,1)S(1)}, u32[]{:S(2)}, u32[]{:S(2)}) collective-permute-start(bf16[256,1024]{1,0:T(8,128)(2,1)} %get-tuple-element.15), channel_id=1, source_target_pairs={{0,8},{8,0},{16,24},{24,16},{1,9},{9,1},{17,25},{25,17},{2,10},{10... | collective-permute-start | bytes 1572872 | tf_op jit(solution)/shard_map/ppermute | solution.py:141
  92.9 2.1 %collective-permute-start.7 = (bf16[256,1024]{1,0:T(8,128)(2,1)}, bf16[256,1024]{1,0:T(8,128)(2,1)S(1)}, u32[]{:S(2)}, u32[]{:S(2)}) collective-permute-start(bf16[256,1024]{1,0:T(8,128)(2,1)} %get-tuple-element.12), channel_id=1, source_target_pairs={{0,8},{8,0},{16,24},{24,16},{1,9},{9,1},{17,25},{25,17},{2,10},{10... | collective-permute-start | bytes 1572872 | tf_op jit(solution)/shard_map/ppermute | solution.py:141
  93.0 9.2 %collective-permute-start.18 = (bf16[128,1024]{1,0:T(8,128)(2,1)S(1)}, bf16[128,1024]{1,0:T(8,128)(2,1)S(1)}, u32[]{:S(2)}, u32[]{:S(2)}) collective-permute-start(bf16[128,1024]{1,0:T(8,128)(2,1)S(1)} %add_convert_fusion), channel_id=1, source_target_pairs={{0,16},{8,24},{16,0},{24,8},{1,17},{9,25},{17,1},{25,9},{2,18},{10... | collective-permute-start | bytes 786440 | tf_op jit(solution)/shard_map/ppermute | solution.py:141
  96.1 11.2 %collective-permute-start.8 = (bf16[128,1024]{1,0:T(8,128)(2,1)S(1)}, bf16[128,1024]{1,0:T(8,128)(2,1)S(1)}, u32[]{:S(2)}, u32[]{:S(2)}) collective-permute-start(bf16[128,1024]{1,0:T(8,128)(2,1)S(1)} %add_convert_fusion.1), channel_id=1, source_target_pairs={{0,16},{8,24},{16,0},{24,8},{1,17},{9,25},{17,1},{25,9},{2,18},{10... | collective-permute-start | bytes 786440 | tf_op jit(solution)/shard_map/ppermute | solution.py:141
  102.4 6.3 %collective-permute-start.19 = (bf16[128,512]{1,0:T(8,128)(2,1)S(1)}, bf16[128,512]{1,0:T(8,128)(2,1)S(1)}, u32[]{:S(2)}, u32[]{:S(2)}) collective-permute-start(bf16[128,512]{1,0:T(8,128)(2,1)S(1)} %slice.106), channel_id=1, source_target_pairs={{0,1},{1,0},{2,3},{3,2},{4,5},{5,4},{6,7},{7,6},{8,9},{9,8},{10,11... | collective-permute-start | bytes 393224 | tf_op jit(solution)/shard_map/ppermute | solution.py:144
  107.5 5.1 %collective-permute-start.9 = (bf16[128,512]{1,0:T(8,128)(2,1)S(1)}, bf16[128,512]{1,0:T(8,128)(2,1)S(1)}, u32[]{:S(2)}, u32[]{:S(2)}) collective-permute-start(bf16[128,512]{1,0:T(8,128)(2,1)S(1)} %slice.107), channel_id=1, source_target_pairs={{0,1},{1,0},{2,3},{3,2},{4,5},{5,4},{6,7},{7,6},{8,9},{9,8},{10,11... | collective-permute-start | bytes 393224 | tf_op jit(solution)/shard_map/ppermute | solution.py:144
  112.7 4.5 %collective-permute-start.20 = (bf16[2,128,128]{2,1,0:T(8,128)(2,1)S(1)}, bf16[2,128,128]{2,1,0:T(8,128)(2,1)S(1)}, u32[]{:S(2)}, u32[]{:S(2)}) collective-permute-start(bf16[2,128,128]{2,1,0:T(8,128)(2,1)S(1)} %get-tuple-element.17), channel_id=1, source_target_pairs={{0,2},{1,3},{2,0},{3,1},{4,6},{5,7},{6,4},{7,5},{8,10},{9,11},{10,... | collective-permute-start | bytes 196616 | tf_op jit(solution)/shard_map/ppermute | solution.py:144
  112.8 5.9 %collective-permute-start.21 = (bf16[2,128,128]{2,1,0:T(8,128)(2,1)S(1)}, bf16[2,128,128]{2,1,0:T(8,128)(2,1)S(1)}, u32[]{:S(2)}, u32[]{:S(2)}) collective-permute-start(bf16[2,128,128]{2,1,0:T(8,128)(2,1)S(1)} %get-tuple-element.19), channel_id=1, source_target_pairs={{0,4},{1,5},{2,6},{3,7},{4,0},{5,1},{6,2},{7,3},{8,12},{9,13},{10,... | collective-permute-start | bytes 196616 | tf_op jit(solution)/shard_map/ppermute | solution.py:144
  114.8 6.1 %collective-permute-start.22 = (bf16[2,128,128]{2,1,0:T(8,128)(2,1)S(1)}, bf16[2,128,128]{2,1,0:T(8,128)(2,1)S(1)}, u32[]{:S(2)}, u32[]{:S(2)}) collective-permute-start(bf16[2,128,128]{2,1,0:T(8,128)(2,1)S(1)} %get-tuple-element.18), channel_id=1, source_target_pairs={{0,6},{1,7},{2,4},{3,5},{4,2},{5,3},{6,0},{7,1},{8,14},{9,15},{10,... | collective-permute-start | bytes 196616 | tf_op jit(solution)/shard_map/ppermute | solution.py:144
  (10 other events, 132.8 us)

commit v2 on v0

v2 whole, which is shorter than its diff:
```python
import functools

import jax
import jax.numpy as jnp
from jax import lax
from jax.experimental import pallas as pl
from jax.experimental.pallas import tpu as pltpu
from jax.sharding import PartitionSpec as P


TILE_P = 512
LANES = 128
VMEM_LIMIT = 44 * 2**20


def xor_pairs(size, mask):
    return [(i, i ^ mask) for i in range(size)]


def xor_columns(value, me, width):
    columns = value.shape[1]
    bit = 1
    while bit * width < columns:
        half = bit * width
        flipped = jnp.concatenate(
            [value[:, (k ^ 1) * half : ((k ^ 1) + 1) * half] for k in range(columns // half)], axis=1
        )
        value = jnp.where(lax.broadcast((me & bit) != 0, value.shape), flipped, value)
        bit *= 2
    return value


def fused_kernel(plan, *refs):
    places_in, places_out, vb, cb, tile = plan
    piece_refs = refs[: len(places_in)]
    con_ref, val_ref, scr_ref = refs[len(places_in) : len(places_in) + 3]
    out_refs = refs[len(places_in) + 3 : len(places_in) + 3 + len(places_out)]
    exc, half, acc, terms, held, sems = refs[len(places_in) + 3 + len(places_out) :]
    me_a, me_b = lax.axis_index("pa"), lax.axis_index("pb")
    aligned = cb % LANES == 0
    slots = held.shape[0]
    tiles = scr_ref.shape[0] // tile

    def fetch(step, slot):
        return pltpu.make_async_copy(
            scr_ref.at[pl.ds(pl.multiple_of(step * tile, tile), tile), :], held.at[slot], sems.at[slot]
        )

    def row(rel):
        return pl.ds(pl.multiple_of((me_a ^ rel) * vb, vb), vb)

    def column(rel):
        return pl.ds(pl.multiple_of((me_b ^ rel) * cb, cb), cb)

    for slot in range(slots):
        fetch(slot, slot).start()

    for ref, (blocks, columns) in zip(piece_refs, places_in):
        for i, rel_a in enumerate(blocks):
            rows = slice(i * vb, (i + 1) * vb)
            if aligned:
                for j, rel_b in enumerate(columns):
                    exc[row(rel_a), column(rel_b)] = ref[rows, j * cb : (j + 1) * cb]
            else:
                value = ref[rows, :]
                value = jnp.concatenate(
                    [value[:, columns.index(k) * cb : (columns.index(k) + 1) * cb] for k in range(len(columns))],
                    axis=1,
                )
                exc[row(rel_a), :] = xor_columns(value, me_b, cb)
    half[...] = lax.dot_general(
        exc[...], con_ref[...], (((1,), (1,)), ((), ())), preferred_element_type=jnp.float32
    ).astype(half.dtype)
    acc[...] = jnp.zeros_like(acc)

    def body(step, carry):
        slot = lax.rem(step, slots)
        fetch(step, slot).wait()
        val = val_ref[pl.ds(pl.multiple_of(step * tile, tile), tile), :]
        expanded = jnp.dot(val, half[...], preferred_element_type=jnp.float32)
        weighted = (held[slot].astype(jnp.float32) * expanded).astype(jnp.bfloat16)

        @pl.when(step + slots < tiles)
        def _():
            fetch(step + slots, slot).start()

        acc[...] += lax.dot_general(
            val, weighted, (((0,), (0,)), ((), ())), preferred_element_type=jnp.float32
        )
        return carry

    lax.fori_loop(0, tiles, body, 0)
    terms[...] = jnp.dot(acc[...].astype(jnp.bfloat16), con_ref[...], preferred_element_type=jnp.float32)
    for ref, places in zip(out_refs, places_out):
        for i, (rel_a, columns) in enumerate(places):
            rows = slice(i * vb, (i + 1) * vb)
            if aligned:
                for j, rel_b in enumerate(columns):
                    ref[rows, j * cb : (j + 1) * cb] = terms[row(rel_a), column(rel_b)].astype(ref.dtype)
            else:
                value = xor_columns(terms[row(rel_a), :], me_b, cb)
                ref[rows, :] = jnp.concatenate(
                    [value[:, k * cb : (k + 1) * cb] for k in columns], axis=1
                ).astype(ref.dtype)


def apply_block(pieces, con, val, screened, places_out, dtypes_out, vb, cb):
    np_, nq = screened.shape
    nv, nc = val.shape[1], con.shape[1]
    tile = min(TILE_P, np_)
    slots = min(3, np_ // tile)
    near = pl.BlockSpec(memory_space=pltpu.VMEM)
    shapes = [(len(p) * vb, len(p[0][1]) * cb) for p in places_out]
    flops = 2 * nv * nc * nq * 2 + 4 * np_ * nq * nv
    plan = (tuple(p[1:] for p in pieces), tuple(places_out), vb, cb, tile)
    return pl.pallas_call(
        functools.partial(fused_kernel, plan),
        out_shape=[jax.ShapeDtypeStruct(s, d) for s, d in zip(shapes, dtypes_out)],
        in_specs=[near] * (len(pieces) + 2) + [pl.BlockSpec(memory_space=pltpu.HBM)],
        out_specs=[near] * len(shapes),
        scratch_shapes=[
            pltpu.VMEM((nv, nc), jnp.bfloat16),
            pltpu.VMEM((nv, nq), jnp.bfloat16),
            pltpu.VMEM((nv, nq), jnp.float32),
            pltpu.VMEM((nv, nc), jnp.float32),
            pltpu.VMEM((slots, tile, nq), jnp.bfloat16),
            pltpu.SemaphoreType.DMA((slots,)),
        ],
        compiler_params=pltpu.CompilerParams(vmem_limit_bytes=VMEM_LIMIT),
        cost_estimate=pl.CostEstimate(
            flops=flops, transcendentals=0, bytes_accessed=2 * (np_ * nq + np_ * nv + nq * nc)
        ),
    )(*[p[0] for p in pieces], con, val, screened)


def bring_kernel(far_ref, near_ref, sem):
    copy = pltpu.make_async_copy(far_ref, near_ref, sem)
    copy.start()
    copy.wait()


def bring_near(array):
    return pl.pallas_call(
        bring_kernel,
        out_shape=pltpu.VMEM(array.shape, array.dtype),
        in_specs=[pl.BlockSpec(memory_space=pltpu.HBM)],
        out_specs=pl.BlockSpec(memory_space=pltpu.VMEM),
        scratch_shapes=[pltpu.SemaphoreType.DMA],
        compiler_params=pltpu.CompilerParams(vmem_limit_bytes=2**20),
    )(array)


def solution(mesh):
    na, nb = mesh.shape["pa"], mesh.shape["pb"]
    low_a, high_a = 2, na // 2
    high_b = min(nb, 4)
    low_b = nb // high_b
    plane = [(a, b) for a in range(high_a) for b in range(low_b)]
    plane = sorted(plane, key=lambda p: -((p[0] != 0) + (p[1] != 0)))
    peers = [p for p in plane if p != (0, 0)]
    line_order = list(range(high_b - 1, 0, -1))

    def to_plane(x, peer):
        a, b = peer[0] * low_a, peer[1]
        if b == 0:
            return lax.ppermute(x, "pa", xor_pairs(na, a))
        if a == 0:
            return lax.ppermute(x, "pb", xor_pairs(nb, b))
        pairs = [(i * nb + j, (i ^ a) * nb + (j ^ b)) for i in range(na) for j in range(nb)]
        return lax.ppermute(x, ("pa", "pb"), pairs)

    def to_core(x, k):
        return lax.ppermute(x, "pa", xor_pairs(na, k))

    def to_line(x, k):
        return lax.ppermute(x, "pb", xor_pairs(nb, k * low_b))

    def local(excitons, screened, phi_val, phi_con):
        count = excitons.shape[0]
        vb, cb = excitons.shape[1:]
        f32, bf16 = jnp.float32, jnp.bfloat16
        wide = high_b * cb
        split = cb % LANES == 0

        def columns(b):
            return tuple(h * low_b + b for h in range(high_b))

        full = sum((columns(b) for b in range(low_b)), ())

        con_near = bring_near(phi_con)
        val_near = bring_near(phi_val)

        arrived = {0: excitons}
        for k in line_order:
            arrived[k] = to_line(excitons, k)
        gathered = []
        for e in range(count):
            line = jnp.concatenate([arrived[k][e] for k in range(high_b)], axis=1)
            early = split and e > 0
            if early:
                line = jnp.concatenate([line] + [to_core(line, c) for c in range(1, low_a)], axis=0)
            got = {(0, 0): line}
            for peer in peers:
                got[peer] = to_plane(line, peer)
            pieces = []
            if early:
                for a, b in plane:
                    blocks = tuple(a * low_a + c for c in range(low_a))
                    pieces.append((got[a, b], blocks, columns(b)))
            else:
                for c in range(low_a):
                    for a in range(high_a):
                        parts = [got[a, b] for b in range(low_b)]
                        if not split:
                            row = jnp.concatenate(parts, axis=1)
                            pieces.append((to_core(row, c) if c else row, (a * low_a + c,), full))
                        else:
                            for b in range(low_b):
                                moved = to_core(parts[b], c) if c else parts[b]
                                pieces.append((moved, (a * low_a + c,), columns(b)))
            gathered.append(pieces)

        sent_places = [
            tuple((a * low_a + c, full) for a in range(high_a)) for c in range(1, low_a)
        ]
        totals = []
        for e in range(count):
            early = split and e < count - 1
            if early:
                places = [tuple((a * low_a + c, columns(b)) for c in range(low_a)) for a, b in plane]
                types = [f32 if p == (0, 0) else bf16 for p in plane]
            elif split:
                places = [((a * low_a, columns(b)),) for a, b in plane] + sent_places
                types = [f32] * len(plane) + [bf16] * len(sent_places)
            else:
                places = [((a * low_a, full),) for a in range(high_a)] + sent_places
                types = [f32] * high_a + [bf16] * len(sent_places)
            outs = apply_block(
                gathered[e], con_near, val_near, screened, places, types, vb, cb
            )
            if early:
                local_sums = dict(zip(plane, outs))
                whole = local_sums[0, 0]
                for peer in peers:
                    whole = whole + to_plane(local_sums[peer], peer).astype(f32)
                own = whole[:vb]
                for c in range(1, low_a):
                    own = own + to_core(whole[c * vb : (c + 1) * vb].astype(bf16), c).astype(f32)
                totals.append(own)
                continue
            kept = outs[: len(outs) - len(sent_places)]
            other = [to_core(x, c + 1).astype(f32) for c, x in enumerate(outs[len(kept) :])]
            total = {}
            for a, b in plane:
                if split:
                    part = kept[plane.index((a, b))]
                else:
                    part = kept[a][:, b * wide : (b + 1) * wide]
                for x in other:
                    part = part + x[a * vb : (a + 1) * vb, b * wide : (b + 1) * wide]
                total[a, b] = part
            whole = total[0, 0]
            for peer in peers:
                whole = whole + to_plane(total[peer].astype(bf16), peer).astype(f32)
            totals.append(whole)
        results = []
        for whole in totals:
            final = whole[:, :cb]
            for k in line_order:
                final = final + to_line(whole[:, k * cb : (k + 1) * cb].astype(bf16), k).astype(f32)
            results.append(final)
        return jnp.stack(results).astype(bf16)

    placed = (P(None, "pa", "pb"), P("pa", "pb"), P("pa", None), P("pb", None))
    return jax.shard_map(local, mesh=mesh, in_specs=placed, out_specs=P(None, "pa", "pb"), check_vma=False)
```

time: 261 us -> 108 us (0.41)
  waiting for transfers between devices: 115 us -> 16.5 us
  matrix products: 80.8 us -> 0 us
  Pallas kernels: 0 us -> 53.8 us
  blocking collectives: 31.1 us -> 0 us
  starting transfers between devices: 0.09 us -> 28.7 us
  other arithmetic: 20.4 us -> 1.28 us
  between operations: 13.1 us -> 0.2 us
  local copies, waits for them, and re-layouts: 0.01 us -> 6.95 us
    reduce_scatter x2 -> x0, waiting for transfers between devices: 113 us -> none  [the longest x1 88.8 us: local(): columns = lax.psum_scatter(terms, 'pb', scatter_dimension=2, tiled=True)]
    dot_general x4 -> x0, matrix products: 80.8 us -> none  [the longest x1 33.7 us: local(): jnp.einsum('pv,evq->epq', phi_val, half_exp, preferred_element_type=jnp.f...]
    pallas_call x0 -> x4, Pallas kernels: none -> 53.8 us  [the longest x2 53.3 us: apply_block(): pl.pallas_call(functools.partial(fused_kernel, plan), out_shape=[jax.Shap...]
    all_gather x1 -> x0, blocking collectives: 31.1 us -> none  [local(): val_rows = lax.all_gather(excitons, 'pb', axis=2, tiled=True)]
    ppermute x0 -> x28, starting transfers between devices: none -> 28.7 us  [the longest x9 13.3 us: to_line(): return lax.ppermute(x, 'pb', xor_pairs(nb, k * low_b))]
    convert_element_type x2, other arithmetic: 20.4 us -> 0.28 us  [the longest x1 0.18 us: local(): whole = whole + to_plane(total[peer].astype(bf16), peer).astype(f32)]
    ppermute x0 -> x28, waiting for transfers between devices: none -> 16.5 us  [the longest x9 7.74 us: to_line(): return lax.ppermute(x, 'pb', xor_pairs(nb, k * low_b))]
    unnamed x2 -> x6, local copies, waits for them, and re-layouts: 0.01 us -> 6.04 us
  transfers between devices with their start and end apart: 3 -> 28, of which waited for: 3 -> 11; matrix products, arithmetic and copies ran while one was open for 7% -> 1% of each run, Pallas kernels for 0% -> 50%
where the time goes in v2:
time: 108 us; the launch traced here: 107 us
  Pallas kernels  53.8 us (50%)
  starting transfers between devices  28.7 us (27%)
  waiting for transfers between devices  16.5 us (15%)
  local copies, waits for them, and re-layouts  6.95 us (6%)
  other arithmetic  1.28 us (1%)
    pallas_call x2, Pallas kernels, apply_block(): pl.pallas_call(functools.partial(fused_kernel, plan), out_shape=[jax.Shap...  53.3 us
    ppermute x9, starting transfers between devices, to_line(): return lax.ppermute(x, 'pb', xor_pairs(nb, k * low_b))  13.3 us
    ppermute x9, waiting for transfers between devices, to_line(): return lax.ppermute(x, 'pb', xor_pairs(nb, k * low_b))  7.74 us
    ppermute x4, starting transfers between devices, to_plane(): return lax.ppermute(x, 'pb', xor_pairs(nb, b))  7.69 us
    unnamed x6, local copies, waits for them, and re-layouts  6.04 us
    ppermute x4, starting transfers between devices, to_plane(): return lax.ppermute(x, 'pa', xor_pairs(na, a))  3.8 us
    ppermute x4, waiting for transfers between devices, to_plane(): return lax.ppermute(x, ('pa', 'pb'), pairs)  3 us
    ppermute x4, waiting for transfers between devices, to_plane(): return lax.ppermute(x, 'pb', xor_pairs(nb, b))  2.94 us
  transfers between devices with their start and end apart: 28, of which 11 were waited for; matrix products, arithmetic and copies ran while one was open for 1% of the time, Pallas kernels for 50%

profile of v2, /device:TPU:0, one launch (start us, length us, event | category | flops | bytes accessed | tf_op | source)
XLA Modules:
  0.0 107.4 jit_solution(15184861595351376357)
XLA Ops:
  0.0 3.1 %collective-permute-start = (bf16[2,128,128]{2,1,0:T(8,128)(2,1)}, bf16[2,128,128]{2,1,0:T(8,128)(2,1)S(1)}, u32[]{:S(2)}, u32[]{:S(2)}) collective-permute-start(bf16[2,128,128]{2,1,0:T(8,128)(2,1)} %param.4), channel_id=1, source_target_pairs={{0,2},{1,3},{2,0},{3,1},{4,6},{5,7},{6,4},{7,5},{8,10},{9,11},{10,... | collective-permute-start | bytes 196616 | tf_op jit(solution)/shard_map/ppermute | solution.py:176
  3.1 2.6 %collective-permute-start.1 = (bf16[2,128,128]{2,1,0:T(8,128)(2,1)}, bf16[2,128,128]{2,1,0:T(8,128)(2,1)S(1)}, u32[]{:S(2)}, u32[]{:S(2)}) collective-permute-start(bf16[2,128,128]{2,1,0:T(8,128)(2,1)} %param.4), channel_id=1, source_target_pairs={{0,4},{1,5},{2,6},{3,7},{4,0},{5,1},{6,2},{7,3},{8,12},{9,13},{10,... | collective-permute-start | bytes 196616 | tf_op jit(solution)/shard_map/ppermute | solution.py:176
  6.5 4.0 %collective-permute-done.1 = bf16[2,128,128]{2,1,0:T(8,128)(2,1)S(1)} collective-permute-done((bf16[2,128,128]{2,1,0:T(8,128)(2,1)}, bf16[2,128,128]{2,1,0:T(8,128)(2,1)S(1)}, u32[]{:S(2)}, u32[]{:S(2)}) %collective-permute-start.1) | collective-permute-done | bytes 65568 | tf_op jit(solution)/shard_map/ppermute | solution.py:176
  10.5 1.4 %collective-permute-done.2 = bf16[2,128,128]{2,1,0:T(8,128)(2,1)S(1)} collective-permute-done((bf16[2,128,128]{2,1,0:T(8,128)(2,1)}, bf16[2,128,128]{2,1,0:T(8,128)(2,1)S(1)}, u32[]{:S(2)}, u32[]{:S(2)}) %collective-permute-start.2) | collective-permute-done | bytes 65568 | tf_op jit(solution)/shard_map/ppermute | solution.py:176
  12.0 1.6 %collective-permute-start.3 = (bf16[128,512]{1,0:T(8,128)(2,1)S(1)}, bf16[128,512]{1,0:T(8,128)(2,1)S(1)}, u32[]{:S(2)}, u32[]{:S(2)}) collective-permute-start(bf16[128,512]{1,0:T(8,128)(2,1)S(1)} %pad_maximum_fusion.1.refs_0_), channel_id=1, source_target_pairs={{0,1},{1,0},{2,3},{3,2},{4,5},{5,4},{6,7},{7,6},{8,9},{9,8},{10,11... | collective-permute-start | bytes 393224 | tf_op jit(solution)/shard_map/ppermute | solution.py:168
  13.5 1.5 %collective-permute-start.4 = (bf16[128,512]{1,0:T(8,128)(2,1)S(1)}, bf16[128,512]{1,0:T(8,128)(2,1)S(1)}, u32[]{:S(2)}, u32[]{:S(2)}) collective-permute-start(bf16[128,512]{1,0:T(8,128)(2,1)S(1)} %pad_maximum_fusion.1.refs_0_), channel_id=1, source_target_pairs={{0,16},{8,24},{16,0},{24,8},{1,17},{9,25},{17,1},{25,9},{2,18},{10... | collective-permute-start | bytes 393224 | tf_op jit(solution)/shard_map/ppermute | solution.py:166
  16.1 1.9 %collective-permute-done.3.refs_1_ = bf16[128,512]{1,0:T(8,128)(2,1)S(1)} collective-permute-done((bf16[128,512]{1,0:T(8,128)(2,1)S(1)}, bf16[128,512]{1,0:T(8,128)(2,1)S(1)}, u32[]{:S(2)}, u32[]{:S(2)}) %collective-permute-start.3) | collective-permute-done | bytes 131104 | tf_op jit(solution)/shard_map/ppermute | solution.py:168
  18.0 1.2 %collective-permute-done.4.refs_2_ = bf16[128,512]{1,0:T(8,128)(2,1)S(1)} collective-permute-done((bf16[128,512]{1,0:T(8,128)(2,1)S(1)}, bf16[128,512]{1,0:T(8,128)(2,1)S(1)}, u32[]{:S(2)}, u32[]{:S(2)}) %collective-permute-start.4) | collective-permute-done | bytes 131104 | tf_op jit(solution)/shard_map/ppermute | solution.py:166
  19.3 1.7 %collective-permute-done.5.refs_3_ = bf16[128,512]{1,0:T(8,128)(2,1)S(1)} collective-permute-done((bf16[128,512]{1,0:T(8,128)(2,1)S(1)}, bf16[128,512]{1,0:T(8,128)(2,1)S(1)}, u32[]{:S(2)}, u32[]{:S(2)}) %collective-permute-start.5) | collective-permute-done | bytes 131104 | tf_op jit(solution)/shard_map/ppermute | solution.py:170
  20.9 2.2 %copy-done = bf16[2048,1024]{1,0:T(8,128)(2,1)S(1)} copy-done((bf16[2048,1024]{1,0:T(8,128)(2,1)S(1)}, bf16[2048,1024]{1,0:T(8,128)(2,1)}, u32[]{:S(2)}) %copy-start) | copy-done | bytes 4194328
  23.4 1.9 %copy-done.1 = bf16[4096,512]{1,0:T(8,128)(2,1)S(1)} copy-done((bf16[4096,512]{1,0:T(8,128)(2,1)S(1)}, bf16[4096,512]{1,0:T(8,128)(2,1)}, u32[]{:S(2)}) %copy-start.1) | copy-done | bytes 4194328
  25.6 2.0 %copy-done.2 = bf16[4096,512]{1,0:T(8,128)(2,1)} copy-done((bf16[4096,512]{1,0:T(8,128)(2,1)}, bf16[4096,512]{1,0:T(8,128)(2,1)S(1)}, u32[]{:S(2)}) %copy-start.2) | copy-done | bytes 4194328
  28.1 2.3 %collective-permute-start.19 = (bf16[256,512]{1,0:T(8,128)(2,1)S(1)}, bf16[256,512]{1,0:T(8,128)(2,1)S(1)}, u32[]{:S(2)}, u32[]{:S(2)}) collective-permute-start(bf16[256,512]{1,0:T(8,128)(2,1)S(1)} %pad_maximum_fusion.refs_3_), channel_id=1, source_target_pairs={{0,1},{1,0},{2,3},{3,2},{4,5},{5,4},{6,7},{7,6},{8,9},{9,8},{10,11... | collective-permute-start | bytes 786440 | tf_op jit(solution)/shard_map/ppermute | solution.py:168
  31.2 26.6 %shard_map.48 = (bf16[256,512]{1,0:T(8,128)(2,1)S(1)}, bf16[256,512]{1,0:T(8,128)(2,1)S(1)}, bf16[256,512]{1,0:T(8,128)(2,1)S(1)}, f32[256,512]{1,0:T(8,128)S(1)}) custom-call(bf16[128,512]{1,0:T(8,128)(2,1)S(1)} %pad_maximum_fusion.1.refs_0_, bf16[128,512]{1,0:T(8,128)(2,1)S(1)} %collective-permute-done.3.refs_1_, ...), custom_call_target="tpu_custom_call" | custom-call | flops 21474836480 | bytes 25165824 | tf_op jit(solution)/shard_map/pallas_call | solution.py:116
  58.6 1.9 %collective-permute-start.11 = (bf16[256,512]{1,0:T(8,128)(2,1)S(1)}, bf16[256,512]{1,0:T(8,128)(2,1)S(1)}, u32[]{:S(2)}, u32[]{:S(2)}) collective-permute-start(bf16[256,512]{1,0:T(8,128)(2,1)S(1)} %get-tuple-element.16), channel_id=1, source_target_pairs={{0,1},{1,0},{2,3},{3,2},{4,5},{5,4},{6,7},{7,6},{8,9},{9,8},{10,11... | collective-permute-start | bytes 786440 | tf_op jit(solution)/shard_map/ppermute | solution.py:168
  61.3 26.7 %shard_map.49 = (f32[128,512]{1,0:T(8,128)S(1)}, f32[128,512]{1,0:T(8,128)S(1)}, f32[128,512]{1,0:T(8,128)S(1)}, f32[128,512]{1,0:T(8,128)S(1)}, bf16[256,1024]{1,0:T(8,128)(2,1)S(1)}) custom-call(bf16[256,512]{1,0:T(8,128)(2,1)S(1)} %collective-permute-done.18.refs_0_, bf16[256,512]{1,0:T(8,128)(2,1)S(1)} %collective-permute-done.19.refs_1_, ...), custom_call_target="tpu_custom_call" | custom-call | flops 21474836480 | bytes 25165824 | tf_op jit(solution)/shard_map/pallas_call | solution.py:116
  88.8 1.3 %collective-permute-done.13 = bf16[128,512]{1,0:T(8,128)(2,1)S(1)} collective-permute-done((bf16[128,512]{1,0:T(8,128)(2,1)S(1)}, bf16[128,512]{1,0:T(8,128)(2,1)S(1)}, u32[]{:S(2)}, u32[]{:S(2)}) %collective-permute-start.13) | collective-permute-done | bytes 131104 | tf_op jit(solution)/shard_map/ppermute | solution.py:173
  91.4 1.9 %collective-permute-start.23 = (bf16[128,512]{1,0:T(8,128)(2,1)S(1)}, bf16[128,512]{1,0:T(8,128)(2,1)S(1)}, u32[]{:S(2)}, u32[]{:S(2)}) collective-permute-start(bf16[128,512]{1,0:T(8,128)(2,1)S(1)} %get-tuple-element.29), channel_id=1, source_target_pairs={{0,1},{1,0},{2,3},{3,2},{4,5},{5,4},{6,7},{7,6},{8,9},{9,8},{10,11... | collective-permute-start | bytes 393224 | tf_op jit(solution)/shard_map/ppermute | solution.py:168
  94.1 1.9 %collective-permute-start.14 = (bf16[128,128]{1,0:T(8,128)(2,1)S(1)}, bf16[128,128]{1,0:T(8,128)(2,1)S(1)}, u32[]{:S(2)}, u32[]{:S(2)}) collective-permute-start(bf16[128,128]{1,0:T(8,128)(2,1)S(1)} %get-tuple-element.30), channel_id=1, source_target_pairs={{0,6},{1,7},{2,4},{3,5},{4,2},{5,3},{6,0},{7,1},{8,14},{9,15},{10,... | collective-permute-start | bytes 98312 | tf_op jit(solution)/shard_map/ppermute | solution.py:176
  96.5 1.3 %collective-permute-done.22 = bf16[128,512]{1,0:T(8,128)(2,1)S(1)} collective-permute-done((bf16[128,512]{1,0:T(8,128)(2,1)S(1)}, bf16[128,512]{1,0:T(8,128)(2,1)S(1)}, u32[]{:S(2)}, u32[]{:S(2)}) %collective-permute-start.22) | collective-permute-done | bytes 131104 | tf_op jit(solution)/shard_map/ppermute | solution.py:170
  98.6 1.0 collective-permute-done.23
  100.0 1.9 %collective-permute-start.25 = (bf16[128,128]{1,0:T(8,128)(2,1)S(1)}, bf16[128,128]{1,0:T(8,128)(2,1)S(1)}, u32[]{:S(2)}, u32[]{:S(2)}) collective-permute-start(bf16[128,128]{1,0:T(8,128)(2,1)S(1)} %get-tuple-element.33), channel_id=1, source_target_pairs={{0,6},{1,7},{2,4},{3,5},{4,2},{5,3},{6,0},{7,1},{8,14},{9,15},{10,... | collective-permute-start | bytes 98312 | tf_op jit(solution)/shard_map/ppermute | solution.py:176
  102.4 2.0 %collective-permute-start.27 = (bf16[128,128]{1,0:T(8,128)(2,1)S(1)}, bf16[128,128]{1,0:T(8,128)(2,1)S(1)}, u32[]{:S(2)}, u32[]{:S(2)}) collective-permute-start(bf16[128,128]{1,0:T(8,128)(2,1)S(1)} %get-tuple-element.34), channel_id=1, source_target_pairs={{0,2},{1,3},{2,0},{3,1},{4,6},{5,7},{6,4},{7,5},{8,10},{9,11},{10,... | collective-permute-start | bytes 98312 | tf_op jit(solution)/shard_map/ppermute | solution.py:176
  104.5 1.7 %collective-permute-done.25 = bf16[128,128]{1,0:T(8,128)(2,1)S(1)} collective-permute-done((bf16[128,128]{1,0:T(8,128)(2,1)S(1)}, bf16[128,128]{1,0:T(8,128)(2,1)S(1)}, u32[]{:S(2)}, u32[]{:S(2)}) %collective-permute-start.25) | collective-permute-done | bytes 32800 | tf_op jit(solution)/shard_map/ppermute | solution.py:176
  (60 shorter events, 11.7 us)
Async XLA Ops:
  0.0 6.5 %collective-permute-start = (bf16[2,128,128]{2,1,0:T(8,128)(2,1)}, bf16[2,128,128]{2,1,0:T(8,128)(2,1)S(1)}, u32[]{:S(2)}, u32[]{:S(2)}) collective-permute-start(bf16[2,128,128]{2,1,0:T(8,128)(2,1)} %param.4), channel_id=1, source_target_pairs={{0,2},{1,3},{2,0},{3,1},{4,6},{5,7},{6,4},{7,5},{8,10},{9,11},{10,... | collective-permute-start | bytes 196616 | tf_op jit(solution)/shard_map/ppermute | solution.py:176
  3.1 7.5 %collective-permute-start.1 = (bf16[2,128,128]{2,1,0:T(8,128)(2,1)}, bf16[2,128,128]{2,1,0:T(8,128)(2,1)S(1)}, u32[]{:S(2)}, u32[]{:S(2)}) collective-permute-start(bf16[2,128,128]{2,1,0:T(8,128)(2,1)} %param.4), channel_id=1, source_target_pairs={{0,4},{1,5},{2,6},{3,7},{4,0},{5,1},{6,2},{7,3},{8,12},{9,13},{10,... | collective-permute-start | bytes 196616 | tf_op jit(solution)/shard_map/ppermute | solution.py:176
  5.6 6.3 %collective-permute-start.2 = (bf16[2,128,128]{2,1,0:T(8,128)(2,1)}, bf16[2,128,128]{2,1,0:T(8,128)(2,1)S(1)}, u32[]{:S(2)}, u32[]{:S(2)}) collective-permute-start(bf16[2,128,128]{2,1,0:T(8,128)(2,1)} %param.4), channel_id=1, source_target_pairs={{0,6},{1,7},{2,4},{3,5},{4,2},{5,3},{6,0},{7,1},{8,14},{9,15},{10,... | collective-permute-start | bytes 196616 | tf_op jit(solution)/shard_map/ppermute | solution.py:176
  12.0 6.1 %collective-permute-start.3 = (bf16[128,512]{1,0:T(8,128)(2,1)S(1)}, bf16[128,512]{1,0:T(8,128)(2,1)S(1)}, u32[]{:S(2)}, u32[]{:S(2)}) collective-permute-start(bf16[128,512]{1,0:T(8,128)(2,1)S(1)} %pad_maximum_fusion.1.refs_0_), channel_id=1, source_target_pairs={{0,1},{1,0},{2,3},{3,2},{4,5},{5,4},{6,7},{7,6},{8,9},{9,8},{10,11... | collective-permute-start | bytes 393224 | tf_op jit(solution)/shard_map/ppermute | solution.py:168
  13.5 5.7 %collective-permute-start.4 = (bf16[128,512]{1,0:T(8,128)(2,1)S(1)}, bf16[128,512]{1,0:T(8,128)(2,1)S(1)}, u32[]{:S(2)}, u32[]{:S(2)}) collective-permute-start(bf16[128,512]{1,0:T(8,128)(2,1)S(1)} %pad_maximum_fusion.1.refs_0_), channel_id=1, source_target_pairs={{0,16},{8,24},{16,0},{24,8},{1,17},{9,25},{17,1},{25,9},{2,18},{10... | collective-permute-start | bytes 393224 | tf_op jit(solution)/shard_map/ppermute | solution.py:166
  15.0 5.9 %collective-permute-start.5 = (bf16[128,512]{1,0:T(8,128)(2,1)S(1)}, bf16[128,512]{1,0:T(8,128)(2,1)S(1)}, u32[]{:S(2)}, u32[]{:S(2)}) collective-permute-start(bf16[128,512]{1,0:T(8,128)(2,1)S(1)} %pad_maximum_fusion.1.refs_0_), channel_id=1, source_target_pairs={{0,17},{1,16},{2,19},{3,18},{4,21},{5,20},{6,23},{7,22},{8,25},{9,... | collective-permute-start | bytes 393224 | tf_op jit(solution)/shard_map/ppermute | solution.py:170
  15.5 12.0 %collective-permute-start.17 = (bf16[128,512]{1,0:T(8,128)(2,1)S(1)}, bf16[128,512]{1,0:T(8,128)(2,1)S(1)}, u32[]{:S(2)}, u32[]{:S(2)}) collective-permute-start(bf16[128,512]{1,0:T(8,128)(2,1)S(1)} %pad_maximum_fusion.2), channel_id=1, source_target_pairs={{0,8},{8,0},{16,24},{24,16},{1,9},{9,1},{17,25},{25,17},{2,10},{10... | collective-permute-start | bytes 393224 | tf_op jit(solution)/shard_map/ppermute | solution.py:173
  15.6 12.5 %collective-permute-start.6 = (bf16[128,512]{1,0:T(8,128)(2,1)S(1)}, bf16[128,512]{1,0:T(8,128)(2,1)S(1)}, u32[]{:S(2)}, u32[]{:S(2)}) collective-permute-start(bf16[128,512]{1,0:T(8,128)(2,1)S(1)} %pad_maximum_fusion.1.refs_0_), channel_id=1, source_target_pairs={{0,8},{8,0},{16,24},{24,16},{1,9},{9,1},{17,25},{25,17},{2,10},{10... | collective-permute-start | bytes 393224 | tf_op jit(solution)/shard_map/ppermute | solution.py:173
  18.0 12.4 %collective-permute-start.7 = (bf16[128,512]{1,0:T(8,128)(2,1)S(1)}, bf16[128,512]{1,0:T(8,128)(2,1)S(1)}, u32[]{:S(2)}, u32[]{:S(2)}) collective-permute-start(bf16[128,512]{1,0:T(8,128)(2,1)S(1)} %collective-permute-done.3.refs_1_), channel_id=1, source_target_pairs={{0,8},{8,0},{16,24},{24,16},{1,9},{9,1},{17,25},{25,17},{2,10},{10... | collective-permute-start | bytes 393224 | tf_op jit(solution)/shard_map/ppermute | solution.py:173
  19.3 11.9 %collective-permute-start.8 = (bf16[128,512]{1,0:T(8,128)(2,1)S(1)}, bf16[128,512]{1,0:T(8,128)(2,1)S(1)}, u32[]{:S(2)}, u32[]{:S(2)}) collective-permute-start(bf16[128,512]{1,0:T(8,128)(2,1)S(1)} %collective-permute-done.4.refs_2_), channel_id=1, source_target_pairs={{0,8},{8,0},{16,24},{24,16},{1,9},{9,1},{17,25},{25,17},{2,10},{10... | collective-permute-start | bytes 393224 | tf_op jit(solution)/shard_map/ppermute | solution.py:173
  20.9 10.3 %collective-permute-start.9 = (bf16[128,512]{1,0:T(8,128)(2,1)S(1)}, bf16[128,512]{1,0:T(8,128)(2,1)S(1)}, u32[]{:S(2)}, u32[]{:S(2)}) collective-permute-start(bf16[128,512]{1,0:T(8,128)(2,1)S(1)} %collective-permute-done.5.refs_3_), channel_id=1, source_target_pairs={{0,8},{8,0},{16,24},{24,16},{1,9},{9,1},{17,25},{25,17},{2,10},{10... | collective-permute-start | bytes 393224 | tf_op jit(solution)/shard_map/ppermute | solution.py:173
  27.6 32.9 %collective-permute-start.18 = (bf16[256,512]{1,0:T(8,128)(2,1)S(1)}, bf16[256,512]{1,0:T(8,128)(2,1)S(1)}, u32[]{:S(2)}, u32[]{:S(2)}) collective-permute-start(bf16[256,512]{1,0:T(8,128)(2,1)S(1)} %pad_maximum_fusion.refs_3_), channel_id=1, source_target_pairs={{0,17},{1,16},{2,19},{3,18},{4,21},{5,20},{6,23},{7,22},{8,25},{9,... | collective-permute-start | bytes 786440 | tf_op jit(solution)/shard_map/ppermute | solution.py:170
  28.1 33.1 %collective-permute-start.19 = (bf16[256,512]{1,0:T(8,128)(2,1)S(1)}, bf16[256,512]{1,0:T(8,128)(2,1)S(1)}, u32[]{:S(2)}, u32[]{:S(2)}) collective-permute-start(bf16[256,512]{1,0:T(8,128)(2,1)S(1)} %pad_maximum_fusion.refs_3_), channel_id=1, source_target_pairs={{0,1},{1,0},{2,3},{3,2},{4,5},{5,4},{6,7},{7,6},{8,9},{9,8},{10,11... | collective-permute-start | bytes 786440 | tf_op jit(solution)/shard_map/ppermute | solution.py:168
  30.4 30.9 %collective-permute-start.20 = (bf16[256,512]{1,0:T(8,128)(2,1)S(1)}, bf16[256,512]{1,0:T(8,128)(2,1)S(1)}, u32[]{:S(2)}, u32[]{:S(2)}) collective-permute-start(bf16[256,512]{1,0:T(8,128)(2,1)S(1)} %pad_maximum_fusion.refs_3_), channel_id=1, source_target_pairs={{0,16},{8,24},{16,0},{24,8},{1,17},{9,25},{17,1},{25,9},{2,18},{10... | collective-permute-start | bytes 786440 | tf_op jit(solution)/shard_map/ppermute | solution.py:166
  57.7 30.4 %collective-permute-start.10 = (bf16[256,512]{1,0:T(8,128)(2,1)S(1)}, bf16[256,512]{1,0:T(8,128)(2,1)S(1)}, u32[]{:S(2)}, u32[]{:S(2)}) collective-permute-start(bf16[256,512]{1,0:T(8,128)(2,1)S(1)} %get-tuple-element.15), channel_id=1, source_target_pairs={{0,17},{1,16},{2,19},{3,18},{4,21},{5,20},{6,23},{7,22},{8,25},{9,... | collective-permute-start | bytes 786440 | tf_op jit(solution)/shard_map/ppermute | solution.py:170
  58.6 29.5 %collective-permute-start.11 = (bf16[256,512]{1,0:T(8,128)(2,1)S(1)}, bf16[256,512]{1,0:T(8,128)(2,1)S(1)}, u32[]{:S(2)}, u32[]{:S(2)}) collective-permute-start(bf16[256,512]{1,0:T(8,128)(2,1)S(1)} %get-tuple-element.16), channel_id=1, source_target_pairs={{0,1},{1,0},{2,3},{3,2},{4,5},{5,4},{6,7},{7,6},{8,9},{9,8},{10,11... | collective-permute-start | bytes 786440 | tf_op jit(solution)/shard_map/ppermute | solution.py:168
  60.5 27.6 %collective-permute-start.12 = (bf16[256,512]{1,0:T(8,128)(2,1)S(1)}, bf16[256,512]{1,0:T(8,128)(2,1)S(1)}, u32[]{:S(2)}, u32[]{:S(2)}) collective-permute-start(bf16[256,512]{1,0:T(8,128)(2,1)S(1)} %get-tuple-element.17), channel_id=1, source_target_pairs={{0,16},{8,24},{16,0},{24,8},{1,17},{9,25},{17,1},{25,9},{2,18},{10... | collective-permute-start | bytes 786440 | tf_op jit(solution)/shard_map/ppermute | solution.py:166
  90.5 7.3 %collective-permute-start.22 = (bf16[128,512]{1,0:T(8,128)(2,1)S(1)}, bf16[128,512]{1,0:T(8,128)(2,1)S(1)}, u32[]{:S(2)}, u32[]{:S(2)}) collective-permute-start(bf16[128,512]{1,0:T(8,128)(2,1)S(1)} %get-tuple-element.27), channel_id=1, source_target_pairs={{0,17},{1,16},{2,19},{3,18},{4,21},{5,20},{6,23},{7,22},{8,25},{9,... | collective-permute-start | bytes 393224 | tf_op jit(solution)/shard_map/ppermute | solution.py:170
  91.4 8.3 %collective-permute-start.23 = (bf16[128,512]{1,0:T(8,128)(2,1)S(1)}, bf16[128,512]{1,0:T(8,128)(2,1)S(1)}, u32[]{:S(2)}, u32[]{:S(2)}) collective-permute-start(bf16[128,512]{1,0:T(8,128)(2,1)S(1)} %get-tuple-element.29), channel_id=1, source_target_pairs={{0,1},{1,0},{2,3},{3,2},{4,5},{5,4},{6,7},{7,6},{8,9},{9,8},{10,11... | collective-permute-start | bytes 393224 | tf_op jit(solution)/shard_map/ppermute | solution.py:168
  93.3 6.5 %collective-permute-start.24 = (bf16[128,512]{1,0:T(8,128)(2,1)S(1)}, bf16[128,512]{1,0:T(8,128)(2,1)S(1)}, u32[]{:S(2)}, u32[]{:S(2)}) collective-permute-start(bf16[128,512]{1,0:T(8,128)(2,1)S(1)} %get-tuple-element.28), channel_id=1, source_target_pairs={{0,16},{8,24},{16,0},{24,8},{1,17},{9,25},{17,1},{25,9},{2,18},{10... | collective-permute-start | bytes 393224 | tf_op jit(solution)/shard_map/ppermute | solution.py:166
  94.1 8.3 %collective-permute-start.14 = (bf16[128,128]{1,0:T(8,128)(2,1)S(1)}, bf16[128,128]{1,0:T(8,128)(2,1)S(1)}, u32[]{:S(2)}, u32[]{:S(2)}) collective-permute-start(bf16[128,128]{1,0:T(8,128)(2,1)S(1)} %get-tuple-element.30), channel_id=1, source_target_pairs={{0,6},{1,7},{2,4},{3,5},{4,2},{5,3},{6,0},{7,1},{8,14},{9,15},{10,... | collective-permute-start | bytes 98312 | tf_op jit(solution)/shard_map/ppermute | solution.py:176
  96.0 8.4 %collective-permute-start.15 = (bf16[128,128]{1,0:T(8,128)(2,1)S(1)}, bf16[128,128]{1,0:T(8,128)(2,1)S(1)}, u32[]{:S(2)}, u32[]{:S(2)}) collective-permute-start(bf16[128,128]{1,0:T(8,128)(2,1)S(1)} %get-tuple-element.32), channel_id=1, source_target_pairs={{0,4},{1,5},{2,6},{3,7},{4,0},{5,1},{6,2},{7,3},{8,12},{9,13},{10,... | collective-permute-start | bytes 98312 | tf_op jit(solution)/shard_map/ppermute | solution.py:176
  97.9 6.6 %collective-permute-start.16 = (bf16[128,128]{1,0:T(8,128)(2,1)S(1)}, bf16[128,128]{1,0:T(8,128)(2,1)S(1)}, u32[]{:S(2)}, u32[]{:S(2)}) collective-permute-start(bf16[128,128]{1,0:T(8,128)(2,1)S(1)} %get-tuple-element.31), channel_id=1, source_target_pairs={{0,2},{1,3},{2,0},{3,1},{4,6},{5,7},{6,4},{7,5},{8,10},{9,11},{10,... | collective-permute-start | bytes 98312 | tf_op jit(solution)/shard_map/ppermute | solution.py:176
  100.0 6.1 %collective-permute-start.25 = (bf16[128,128]{1,0:T(8,128)(2,1)S(1)}, bf16[128,128]{1,0:T(8,128)(2,1)S(1)}, u32[]{:S(2)}, u32[]{:S(2)}) collective-permute-start(bf16[128,128]{1,0:T(8,128)(2,1)S(1)} %get-tuple-element.33), channel_id=1, source_target_pairs={{0,6},{1,7},{2,4},{3,5},{4,2},{5,3},{6,0},{7,1},{8,14},{9,15},{10,... | collective-permute-start | bytes 98312 | tf_op jit(solution)/shard_map/ppermute | solution.py:176
  (7 other events, 19.7 us)

commit v3 on v2

--- a/solution.py
+++ b/solution.py
@@ -8,7 +8,7 @@
 from jax.sharding import PartitionSpec as P
 
 
-TILE_P = 512
+TILE_P = 1024
 LANES = 128
 VMEM_LIMIT = 44 * 2**20
 
@@ -31,11 +31,13 @@
 
 
 def fused_kernel(plan, *refs):
-    places_in, places_out, vb, cb, tile = plan
+    places_in, places_out, deferred, vb, cb, tile = plan
     piece_refs = refs[: len(places_in)]
     con_ref, val_ref, scr_ref = refs[len(places_in) : len(places_in) + 3]
-    out_refs = refs[len(places_in) + 3 : len(places_in) + 3 + len(places_out)]
-    exc, half, acc, terms, held, sems = refs[len(places_in) + 3 + len(places_out) :]
+    given = len(places_in) + 3
+    outs = len(places_out) + bool(deferred)
+    out_refs = refs[given : given + outs]
+    exc, half, acc, terms, held, sems = refs[given + outs :]
     me_a, me_b = lax.axis_index("pa"), lax.axis_index("pb")
     aligned = cb % LANES == 0
     slots = held.shape[0]
@@ -90,6 +92,19 @@
         return carry
 
     lax.fori_loop(0, tiles, body, 0)
+    if deferred:
+        send_ref, back_ref = out_refs
+        height = len(places_out[0]) * vb
+        for i, (rel_a, _) in enumerate(places_out[0]):
+            half[i * vb : (i + 1) * vb, :] = acc[row(rel_a), :].astype(half.dtype)
+        for i, rel_a in enumerate(deferred):
+            back_ref[i * vb : (i + 1) * vb, :] = acc[row(rel_a), :].astype(back_ref.dtype)
+        terms[:height, :] = jnp.dot(half[:height, :], con_ref[...], preferred_element_type=jnp.float32)
+        for i, (_, columns) in enumerate(places_out[0]):
+            rows = slice(i * vb, (i + 1) * vb)
+            for j, rel_b in enumerate(columns):
+                send_ref[rows, j * cb : (j + 1) * cb] = terms[rows, column(rel_b)].astype(send_ref.dtype)
+        return
     terms[...] = jnp.dot(acc[...].astype(jnp.bfloat16), con_ref[...], preferred_element_type=jnp.float32)
     for ref, places in zip(out_refs, places_out):
         for i, (rel_a, columns) in enumerate(places):
@@ -104,15 +119,45 @@
                 ).astype(ref.dtype)
 
 
-def apply_block(pieces, con, val, screened, places_out, dtypes_out, vb, cb):
+def last_kernel(places_out, vb, cb, back_ref, con_ref, *refs):
+    out_refs, terms = refs[:-1], refs[-1]
+    me_b = lax.axis_index("pb")
+    terms[...] = jnp.dot(back_ref[...], con_ref[...], preferred_element_type=jnp.float32)
+    for ref, (i, columns) in zip(out_refs, places_out):
+        for j, rel_b in enumerate(columns):
+            place = pl.ds(pl.multiple_of((me_b ^ rel_b) * cb, cb), cb)
+            ref[:, j * cb : (j + 1) * cb] = terms[i * vb : (i + 1) * vb, place]
+
+
+def apply_last(back, con, places_out, vb, cb):
+    rows, nc = back.shape[0], con.shape[1]
+    near = pl.BlockSpec(memory_space=pltpu.VMEM)
+    return pl.pallas_call(
+        functools.partial(last_kernel, places_out, vb, cb),
+        out_shape=[jax.ShapeDtypeStruct((vb, len(p[1]) * cb), jnp.float32) for p in places_out],
+        in_specs=[near] * 2,
+        out_specs=[near] * len(places_out),
+        scratch_shapes=[pltpu.VMEM((rows, nc), jnp.float32)],
+        compiler_params=pltpu.CompilerParams(vmem_limit_bytes=VMEM_LIMIT),
+        cost_estimate=pl.CostEstimate(
+            flops=2 * rows * con.shape[0] * nc, transcendentals=0, bytes_accessed=2 * con.size
+        ),
+    )(back, con)
+
+
+def apply_block(pieces, con, val, screened, places_out, dtypes_out, vb, cb, deferred=()):
     np_, nq = screened.shape
     nv, nc = val.shape[1], con.shape[1]
     tile = min(TILE_P, np_)
-    slots = min(3, np_ // tile)
+    slots = min(2, np_ // tile)
     near = pl.BlockSpec(memory_space=pltpu.VMEM)
     shapes = [(len(p) * vb, len(p[0][1]) * cb) for p in places_out]
+    dtypes_out = list(dtypes_out)
+    if deferred:
+        shapes.append((len(deferred) * vb, nq))
+        dtypes_out.append(jnp.bfloat16)
     flops = 2 * nv * nc * nq * 2 + 4 * np_ * nq * nv
-    plan = (tuple(p[1:] for p in pieces), tuple(places_out), vb, cb, tile)
+    plan = (tuple(p[1:] for p in pieces), tuple(places_out), tuple(deferred), vb, cb, tile)
     return pl.pallas_call(
         functools.partial(fused_kernel, plan),
         out_shape=[jax.ShapeDtypeStruct(s, d) for s, d in zip(shapes, dtypes_out)],
@@ -230,13 +275,13 @@
                 places = [tuple((a * low_a + c, columns(b)) for c in range(low_a)) for a, b in plane]
                 types = [f32 if p == (0, 0) else bf16 for p in plane]
             elif split:
-                places = [((a * low_a, columns(b)),) for a, b in plane] + sent_places
-                types = [f32] * len(plane) + [bf16] * len(sent_places)
+                places, types = sent_places, [bf16]
             else:
                 places = [((a * low_a, full),) for a in range(high_a)] + sent_places
                 types = [f32] * high_a + [bf16] * len(sent_places)
             outs = apply_block(
-                gathered[e], con_near, val_near, screened, places, types, vb, cb
+                gathered[e], con_near, val_near, screened, places, types, vb, cb,
+                tuple(a * low_a for a in range(high_a)) if split and not early else (),
             )
             if early:
                 local_sums = dict(zip(plane, outs))
@@ -248,8 +293,12 @@
                     own = own + to_core(whole[c * vb : (c + 1) * vb].astype(bf16), c).astype(f32)
                 totals.append(own)
                 continue
-            kept = outs[: len(outs) - len(sent_places)]
-            other = [to_core(x, c + 1).astype(f32) for c, x in enumerate(outs[len(kept) :])]
+            if split:
+                sent, (back,) = outs[:1], outs[1:]
+                kept = apply_last(back, con_near, tuple((a, columns(b)) for a, b in plane), vb, cb)
+            else:
+                kept, sent = outs[:high_a], outs[high_a:]
+            other = [to_core(x, c + 1).astype(f32) for c, x in enumerate(sent)]
             total = {}
             for a, b in plane:
                 if split:

time: 108 us -> 105 us (0.972)
  waiting for transfers between devices: 16.5 us -> 15.1 us
  Pallas kernels: 53.8 us -> 52.5 us
    pallas_call x2, Pallas kernels: 53.3 us -> 50.5 us  [apply_block(): pl.pallas_call(functools.partial(fused_kernel, plan), out_shape=[jax.Shap...]
    pallas_call x0 -> x1, Pallas kernels: none -> 1.4 us  [apply_last(): pl.pallas_call(functools.partial(last_kernel, places_out, vb, cb), out_sh...]
    ppermute x7, waiting for transfers between devices: 1.36 us -> 0.02 us  [to_core(): return lax.ppermute(x, 'pa', xor_pairs(na, k))]
where the time goes in v3:
time: 105 us
  Pallas kernels  52.5 us (50%)
  starting transfers between devices  28.7 us (27%)
  waiting for transfers between devices  15.1 us (14%)
  local copies, waits for them, and re-layouts  6.96 us (7%)
  other arithmetic  1.27 us (1%)
    pallas_call x2, Pallas kernels, apply_block(): pl.pallas_call(functools.partial(fused_kernel, plan), out_shape=[jax.Shap...  50.5 us
    ppermute x9, starting transfers between devices, to_line(): return lax.ppermute(x, 'pb', xor_pairs(nb, k * low_b))  13.3 us
    ppermute x9, waiting for transfers between devices, to_line(): return lax.ppermute(x, 'pb', xor_pairs(nb, k * low_b))  7.76 us
    ppermute x4, starting transfers between devices, to_plane(): return lax.ppermute(x, 'pb', xor_pairs(nb, b))  7.71 us
    unnamed x6, local copies, waits for them, and re-layouts  6.06 us
    ppermute x4, starting transfers between devices, to_plane(): return lax.ppermute(x, 'pa', xor_pairs(na, a))  3.8 us
    ppermute x4, waiting for transfers between devices, to_plane(): return lax.ppermute(x, ('pa', 'pb'), pairs)  3.01 us
    ppermute x4, waiting for transfers between devices, to_plane(): return lax.ppermute(x, 'pb', xor_pairs(nb, b))  2.86 us
  transfers between devices with their start and end apart: 28, of which 11 were waited for; matrix products, arithmetic and copies ran while one was open for 1% of the time, Pallas kernels for 50%

profile of v3, /device:TPU:0, one launch (start us, length us, event | category | flops | bytes accessed | tf_op | source)
XLA Modules:
  0.0 104.7 jit_solution(6483695532936561906)
XLA Ops:
  0.0 3.1 %collective-permute-start = (bf16[2,128,128]{2,1,0:T(8,128)(2,1)}, bf16[2,128,128]{2,1,0:T(8,128)(2,1)S(1)}, u32[]{:S(2)}, u32[]{:S(2)}) collective-permute-start(bf16[2,128,128]{2,1,0:T(8,128)(2,1)} %param.4), channel_id=1, source_target_pairs={{0,2},{1,3},{2,0},{3,1},{4,6},{5,7},{6,4},{7,5},{8,10},{9,11},{10,... | collective-permute-start | bytes 196616 | tf_op jit(solution)/shard_map/ppermute | solution.py:221
  3.1 2.6 %collective-permute-start.1 = (bf16[2,128,128]{2,1,0:T(8,128)(2,1)}, bf16[2,128,128]{2,1,0:T(8,128)(2,1)S(1)}, u32[]{:S(2)}, u32[]{:S(2)}) collective-permute-start(bf16[2,128,128]{2,1,0:T(8,128)(2,1)} %param.4), channel_id=1, source_target_pairs={{0,4},{1,5},{2,6},{3,7},{4,0},{5,1},{6,2},{7,3},{8,12},{9,13},{10,... | collective-permute-start | bytes 196616 | tf_op jit(solution)/shard_map/ppermute | solution.py:221
  6.5 4.0 %collective-permute-done.1 = bf16[2,128,128]{2,1,0:T(8,128)(2,1)S(1)} collective-permute-done((bf16[2,128,128]{2,1,0:T(8,128)(2,1)}, bf16[2,128,128]{2,1,0:T(8,128)(2,1)S(1)}, u32[]{:S(2)}, u32[]{:S(2)}) %collective-permute-start.1) | collective-permute-done | bytes 65568 | tf_op jit(solution)/shard_map/ppermute | solution.py:221
  10.5 1.4 %collective-permute-done.2 = bf16[2,128,128]{2,1,0:T(8,128)(2,1)S(1)} collective-permute-done((bf16[2,128,128]{2,1,0:T(8,128)(2,1)}, bf16[2,128,128]{2,1,0:T(8,128)(2,1)S(1)}, u32[]{:S(2)}, u32[]{:S(2)}) %collective-permute-start.2) | collective-permute-done | bytes 65568 | tf_op jit(solution)/shard_map/ppermute | solution.py:221
  12.0 1.6 %collective-permute-start.3 = (bf16[128,512]{1,0:T(8,128)(2,1)S(1)}, bf16[128,512]{1,0:T(8,128)(2,1)S(1)}, u32[]{:S(2)}, u32[]{:S(2)}) collective-permute-start(bf16[128,512]{1,0:T(8,128)(2,1)S(1)} %pad_maximum_fusion.1.refs_0_), channel_id=1, source_target_pairs={{0,1},{1,0},{2,3},{3,2},{4,5},{5,4},{6,7},{7,6},{8,9},{9,8},{10,11... | collective-permute-start | bytes 393224 | tf_op jit(solution)/shard_map/ppermute | solution.py:213
  13.5 1.5 %collective-permute-start.4 = (bf16[128,512]{1,0:T(8,128)(2,1)S(1)}, bf16[128,512]{1,0:T(8,128)(2,1)S(1)}, u32[]{:S(2)}, u32[]{:S(2)}) collective-permute-start(bf16[128,512]{1,0:T(8,128)(2,1)S(1)} %pad_maximum_fusion.1.refs_0_), channel_id=1, source_target_pairs={{0,16},{8,24},{16,0},{24,8},{1,17},{9,25},{17,1},{25,9},{2,18},{10... | collective-permute-start | bytes 393224 | tf_op jit(solution)/shard_map/ppermute | solution.py:211
  16.1 1.9 %collective-permute-done.3.refs_1_ = bf16[128,512]{1,0:T(8,128)(2,1)S(1)} collective-permute-done((bf16[128,512]{1,0:T(8,128)(2,1)S(1)}, bf16[128,512]{1,0:T(8,128)(2,1)S(1)}, u32[]{:S(2)}, u32[]{:S(2)}) %collective-permute-start.3) | collective-permute-done | bytes 131104 | tf_op jit(solution)/shard_map/ppermute | solution.py:213
  18.0 1.2 %collective-permute-done.4.refs_2_ = bf16[128,512]{1,0:T(8,128)(2,1)S(1)} collective-permute-done((bf16[128,512]{1,0:T(8,128)(2,1)S(1)}, bf16[128,512]{1,0:T(8,128)(2,1)S(1)}, u32[]{:S(2)}, u32[]{:S(2)}) %collective-permute-start.4) | collective-permute-done | bytes 131104 | tf_op jit(solution)/shard_map/ppermute | solution.py:211
  19.3 1.7 %collective-permute-done.5.refs_3_ = bf16[128,512]{1,0:T(8,128)(2,1)S(1)} collective-permute-done((bf16[128,512]{1,0:T(8,128)(2,1)S(1)}, bf16[128,512]{1,0:T(8,128)(2,1)S(1)}, u32[]{:S(2)}, u32[]{:S(2)}) %collective-permute-start.5) | collective-permute-done | bytes 131104 | tf_op jit(solution)/shard_map/ppermute | solution.py:215
  20.9 2.2 %copy-done = bf16[2048,1024]{1,0:T(8,128)(2,1)S(1)} copy-done((bf16[2048,1024]{1,0:T(8,128)(2,1)S(1)}, bf16[2048,1024]{1,0:T(8,128)(2,1)}, u32[]{:S(2)}) %copy-start) | copy-done | bytes 4194328
  23.4 1.9 %copy-done.1 = bf16[4096,512]{1,0:T(8,128)(2,1)S(1)} copy-done((bf16[4096,512]{1,0:T(8,128)(2,1)S(1)}, bf16[4096,512]{1,0:T(8,128)(2,1)}, u32[]{:S(2)}) %copy-start.1) | copy-done | bytes 4194328
  25.6 2.0 %copy-done.2 = bf16[4096,512]{1,0:T(8,128)(2,1)} copy-done((bf16[4096,512]{1,0:T(8,128)(2,1)}, bf16[4096,512]{1,0:T(8,128)(2,1)S(1)}, u32[]{:S(2)}) %copy-start.2) | copy-done | bytes 4194328
  28.2 2.3 %collective-permute-start.19 = (bf16[256,512]{1,0:T(8,128)(2,1)S(1)}, bf16[256,512]{1,0:T(8,128)(2,1)S(1)}, u32[]{:S(2)}, u32[]{:S(2)}) collective-permute-start(bf16[256,512]{1,0:T(8,128)(2,1)S(1)} %pad_maximum_fusion.refs_3_), channel_id=1, source_target_pairs={{0,1},{1,0},{2,3},{3,2},{4,5},{5,4},{6,7},{7,6},{8,9},{9,8},{10,11... | collective-permute-start | bytes 786440 | tf_op jit(solution)/shard_map/ppermute | solution.py:213
  31.2 25.7 %shard_map.48 = (bf16[256,512]{1,0:T(8,128)(2,1)S(1)}, bf16[256,512]{1,0:T(8,128)(2,1)S(1)}, bf16[256,512]{1,0:T(8,128)(2,1)S(1)}, f32[256,512]{1,0:T(8,128)S(1)}) custom-call(bf16[128,512]{1,0:T(8,128)(2,1)S(1)} %pad_maximum_fusion.1.refs_0_, bf16[128,512]{1,0:T(8,128)(2,1)S(1)} %collective-permute-done.3.refs_1_, ...), custom_call_target="tpu_custom_call" | custom-call | flops 21474836480 | bytes 25165824 | tf_op jit(solution)/shard_map/pallas_call | solution.py:161
  57.8 1.9 %collective-permute-start.11 = (bf16[256,512]{1,0:T(8,128)(2,1)S(1)}, bf16[256,512]{1,0:T(8,128)(2,1)S(1)}, u32[]{:S(2)}, u32[]{:S(2)}) collective-permute-start(bf16[256,512]{1,0:T(8,128)(2,1)S(1)} %get-tuple-element.17), channel_id=1, source_target_pairs={{0,1},{1,0},{2,3},{3,2},{4,5},{5,4},{6,7},{7,6},{8,9},{9,8},{10,11... | collective-permute-start | bytes 786440 | tf_op jit(solution)/shard_map/ppermute | solution.py:213
  60.5 24.8 %shard_map.49 = (bf16[256,1024]{1,0:T(8,128)(2,1)S(1)}, bf16[256,2048]{1,0:T(8,128)(2,1)S(1)}) custom-call(bf16[256,512]{1,0:T(8,128)(2,1)S(1)} %collective-permute-done.18.refs_0_, bf16[256,512]{1,0:T(8,128)(2,1)S(1)} %collective-permute-done.19.refs_1_, bf16[256,512]{1,0:T(8,128)(2,1)S(1)} %collective-permute-done.20.refs_2_, ...), custom_call_target="tpu_custom_call" | custom-call | flops 21474836480 | bytes 25165824 | tf_op jit(solution)/shard_map/pallas_call | solution.py:161
  86.1 1.4 %shard_map.50 = (f32[128,512]{1,0:T(8,128)S(1)}, f32[128,512]{1,0:T(8,128)S(1)}, f32[128,512]{1,0:T(8,128)S(1)}, f32[128,512]{1,0:T(8,128)S(1)}) custom-call(bf16[256,2048]{1,0:T(8,128)(2,1)S(1)} %get-tuple-element.19.back_ref, bf16[2048,1024]{1,0:T(8,128)(2,1)S(1)} %shard_map.46.refs_8_.refs_4_.con_ref), custom_call_target="tpu_custom_call" | custom-call | flops 1073741824 | bytes 4194304 | tf_op jit(solution)/shard_map/pallas_call | solution.py:135
  88.7 2.0 %collective-permute-start.23 = (bf16[128,512]{1,0:T(8,128)(2,1)S(1)}, bf16[128,512]{1,0:T(8,128)(2,1)S(1)}, u32[]{:S(2)}, u32[]{:S(2)}) collective-permute-start(bf16[128,512]{1,0:T(8,128)(2,1)S(1)} %get-tuple-element.31), channel_id=1, source_target_pairs={{0,1},{1,0},{2,3},{3,2},{4,5},{5,4},{6,7},{7,6},{8,9},{9,8},{10,11... | collective-permute-start | bytes 393224 | tf_op jit(solution)/shard_map/ppermute | solution.py:213
  91.5 1.9 %collective-permute-start.14 = (bf16[128,128]{1,0:T(8,128)(2,1)S(1)}, bf16[128,128]{1,0:T(8,128)(2,1)S(1)}, u32[]{:S(2)}, u32[]{:S(2)}) collective-permute-start(bf16[128,128]{1,0:T(8,128)(2,1)S(1)} %get-tuple-element.32), channel_id=1, source_target_pairs={{0,6},{1,7},{2,4},{3,5},{4,2},{5,3},{6,0},{7,1},{8,14},{9,15},{10,... | collective-permute-start | bytes 98312 | tf_op jit(solution)/shard_map/ppermute | solution.py:221
  93.9 1.4 %collective-permute-done.22 = bf16[128,512]{1,0:T(8,128)(2,1)S(1)} collective-permute-done((bf16[128,512]{1,0:T(8,128)(2,1)S(1)}, bf16[128,512]{1,0:T(8,128)(2,1)S(1)}, u32[]{:S(2)}, u32[]{:S(2)}) %collective-permute-start.22) | collective-permute-done | bytes 131104 | tf_op jit(solution)/shard_map/ppermute | solution.py:215
  96.0 1.0 collective-permute-done.23
  97.2 1.9 %collective-permute-start.25 = (bf16[128,128]{1,0:T(8,128)(2,1)S(1)}, bf16[128,128]{1,0:T(8,128)(2,1)S(1)}, u32[]{:S(2)}, u32[]{:S(2)}) collective-permute-start(bf16[128,128]{1,0:T(8,128)(2,1)S(1)} %get-tuple-element.35), channel_id=1, source_target_pairs={{0,6},{1,7},{2,4},{3,5},{4,2},{5,3},{6,0},{7,1},{8,14},{9,15},{10,... | collective-permute-start | bytes 98312 | tf_op jit(solution)/shard_map/ppermute | solution.py:221
  99.7 2.0 %collective-permute-start.27 = (bf16[128,128]{1,0:T(8,128)(2,1)S(1)}, bf16[128,128]{1,0:T(8,128)(2,1)S(1)}, u32[]{:S(2)}, u32[]{:S(2)}) collective-permute-start(bf16[128,128]{1,0:T(8,128)(2,1)S(1)} %get-tuple-element.36), channel_id=1, source_target_pairs={{0,2},{1,3},{2,0},{3,1},{4,6},{5,7},{6,4},{7,5},{8,10},{9,11},{10,... | collective-permute-start | bytes 98312 | tf_op jit(solution)/shard_map/ppermute | solution.py:221
  101.7 1.8 %collective-permute-done.25 = bf16[128,128]{1,0:T(8,128)(2,1)S(1)} collective-permute-done((bf16[128,128]{1,0:T(8,128)(2,1)S(1)}, bf16[128,128]{1,0:T(8,128)(2,1)S(1)}, u32[]{:S(2)}, u32[]{:S(2)}) %collective-permute-start.25) | collective-permute-done | bytes 32800 | tf_op jit(solution)/shard_map/ppermute | solution.py:221
  (61 shorter events, 11.6 us)
Async XLA Ops:
  0.0 6.5 %collective-permute-start = (bf16[2,128,128]{2,1,0:T(8,128)(2,1)}, bf16[2,128,128]{2,1,0:T(8,128)(2,1)S(1)}, u32[]{:S(2)}, u32[]{:S(2)}) collective-permute-start(bf16[2,128,128]{2,1,0:T(8,128)(2,1)} %param.4), channel_id=1, source_target_pairs={{0,2},{1,3},{2,0},{3,1},{4,6},{5,7},{6,4},{7,5},{8,10},{9,11},{10,... | collective-permute-start | bytes 196616 | tf_op jit(solution)/shard_map/ppermute | solution.py:221
  3.1 7.5 %collective-permute-start.1 = (bf16[2,128,128]{2,1,0:T(8,128)(2,1)}, bf16[2,128,128]{2,1,0:T(8,128)(2,1)S(1)}, u32[]{:S(2)}, u32[]{:S(2)}) collective-permute-start(bf16[2,128,128]{2,1,0:T(8,128)(2,1)} %param.4), channel_id=1, source_target_pairs={{0,4},{1,5},{2,6},{3,7},{4,0},{5,1},{6,2},{7,3},{8,12},{9,13},{10,... | collective-permute-start | bytes 196616 | tf_op jit(solution)/shard_map/ppermute | solution.py:221
  5.6 6.3 %collective-permute-start.2 = (bf16[2,128,128]{2,1,0:T(8,128)(2,1)}, bf16[2,128,128]{2,1,0:T(8,128)(2,1)S(1)}, u32[]{:S(2)}, u32[]{:S(2)}) collective-permute-start(bf16[2,128,128]{2,1,0:T(8,128)(2,1)} %param.4), channel_id=1, source_target_pairs={{0,6},{1,7},{2,4},{3,5},{4,2},{5,3},{6,0},{7,1},{8,14},{9,15},{10,... | collective-permute-start | bytes 196616 | tf_op jit(solution)/shard_map/ppermute | solution.py:221
  12.0 6.1 %collective-permute-start.3 = (bf16[128,512]{1,0:T(8,128)(2,1)S(1)}, bf16[128,512]{1,0:T(8,128)(2,1)S(1)}, u32[]{:S(2)}, u32[]{:S(2)}) collective-permute-start(bf16[128,512]{1,0:T(8,128)(2,1)S(1)} %pad_maximum_fusion.1.refs_0_), channel_id=1, source_target_pairs={{0,1},{1,0},{2,3},{3,2},{4,5},{5,4},{6,7},{7,6},{8,9},{9,8},{10,11... | collective-permute-start | bytes 393224 | tf_op jit(solution)/shard_map/ppermute | solution.py:213
  13.5 5.7 %collective-permute-start.4 = (bf16[128,512]{1,0:T(8,128)(2,1)S(1)}, bf16[128,512]{1,0:T(8,128)(2,1)S(1)}, u32[]{:S(2)}, u32[]{:S(2)}) collective-permute-start(bf16[128,512]{1,0:T(8,128)(2,1)S(1)} %pad_maximum_fusion.1.refs_0_), channel_id=1, source_target_pairs={{0,16},{8,24},{16,0},{24,8},{1,17},{9,25},{17,1},{25,9},{2,18},{10... | collective-permute-start | bytes 393224 | tf_op jit(solution)/shard_map/ppermute | solution.py:211
  15.0 5.9 %collective-permute-start.5 = (bf16[128,512]{1,0:T(8,128)(2,1)S(1)}, bf16[128,512]{1,0:T(8,128)(2,1)S(1)}, u32[]{:S(2)}, u32[]{:S(2)}) collective-permute-start(bf16[128,512]{1,0:T(8,128)(2,1)S(1)} %pad_maximum_fusion.1.refs_0_), channel_id=1, source_target_pairs={{0,17},{1,16},{2,19},{3,18},{4,21},{5,20},{6,23},{7,22},{8,25},{9,... | collective-permute-start | bytes 393224 | tf_op jit(solution)/shard_map/ppermute | solution.py:215
  15.5 12.0 %collective-permute-start.17 = (bf16[128,512]{1,0:T(8,128)(2,1)S(1)}, bf16[128,512]{1,0:T(8,128)(2,1)S(1)}, u32[]{:S(2)}, u32[]{:S(2)}) collective-permute-start(bf16[128,512]{1,0:T(8,128)(2,1)S(1)} %pad_maximum_fusion.2), channel_id=1, source_target_pairs={{0,8},{8,0},{16,24},{24,16},{1,9},{9,1},{17,25},{25,17},{2,10},{10... | collective-permute-start | bytes 393224 | tf_op jit(solution)/shard_map/ppermute | solution.py:218
  15.6 12.5 %collective-permute-start.6 = (bf16[128,512]{1,0:T(8,128)(2,1)S(1)}, bf16[128,512]{1,0:T(8,128)(2,1)S(1)}, u32[]{:S(2)}, u32[]{:S(2)}) collective-permute-start(bf16[128,512]{1,0:T(8,128)(2,1)S(1)} %pad_maximum_fusion.1.refs_0_), channel_id=1, source_target_pairs={{0,8},{8,0},{16,24},{24,16},{1,9},{9,1},{17,25},{25,17},{2,10},{10... | collective-permute-start | bytes 393224 | tf_op jit(solution)/shard_map/ppermute | solution.py:218
  18.0 12.4 %collective-permute-start.7 = (bf16[128,512]{1,0:T(8,128)(2,1)S(1)}, bf16[128,512]{1,0:T(8,128)(2,1)S(1)}, u32[]{:S(2)}, u32[]{:S(2)}) collective-permute-start(bf16[128,512]{1,0:T(8,128)(2,1)S(1)} %collective-permute-done.3.refs_1_), channel_id=1, source_target_pairs={{0,8},{8,0},{16,24},{24,16},{1,9},{9,1},{17,25},{25,17},{2,10},{10... | collective-permute-start | bytes 393224 | tf_op jit(solution)/shard_map/ppermute | solution.py:218
  19.3 11.9 %collective-permute-start.8 = (bf16[128,512]{1,0:T(8,128)(2,1)S(1)}, bf16[128,512]{1,0:T(8,128)(2,1)S(1)}, u32[]{:S(2)}, u32[]{:S(2)}) collective-permute-start(bf16[128,512]{1,0:T(8,128)(2,1)S(1)} %collective-permute-done.4.refs_2_), channel_id=1, source_target_pairs={{0,8},{8,0},{16,24},{24,16},{1,9},{9,1},{17,25},{25,17},{2,10},{10... | collective-permute-start | bytes 393224 | tf_op jit(solution)/shard_map/ppermute | solution.py:218
  20.9 10.3 %collective-permute-start.9 = (bf16[128,512]{1,0:T(8,128)(2,1)S(1)}, bf16[128,512]{1,0:T(8,128)(2,1)S(1)}, u32[]{:S(2)}, u32[]{:S(2)}) collective-permute-start(bf16[128,512]{1,0:T(8,128)(2,1)S(1)} %collective-permute-done.5.refs_3_), channel_id=1, source_target_pairs={{0,8},{8,0},{16,24},{24,16},{1,9},{9,1},{17,25},{25,17},{2,10},{10... | collective-permute-start | bytes 393224 | tf_op jit(solution)/shard_map/ppermute | solution.py:218
  27.6 32.1 %collective-permute-start.18 = (bf16[256,512]{1,0:T(8,128)(2,1)S(1)}, bf16[256,512]{1,0:T(8,128)(2,1)S(1)}, u32[]{:S(2)}, u32[]{:S(2)}) collective-permute-start(bf16[256,512]{1,0:T(8,128)(2,1)S(1)} %pad_maximum_fusion.refs_3_), channel_id=1, source_target_pairs={{0,17},{1,16},{2,19},{3,18},{4,21},{5,20},{6,23},{7,22},{8,25},{9,... | collective-permute-start | bytes 786440 | tf_op jit(solution)/shard_map/ppermute | solution.py:215
  28.2 32.3 %collective-permute-start.19 = (bf16[256,512]{1,0:T(8,128)(2,1)S(1)}, bf16[256,512]{1,0:T(8,128)(2,1)S(1)}, u32[]{:S(2)}, u32[]{:S(2)}) collective-permute-start(bf16[256,512]{1,0:T(8,128)(2,1)S(1)} %pad_maximum_fusion.refs_3_), channel_id=1, source_target_pairs={{0,1},{1,0},{2,3},{3,2},{4,5},{5,4},{6,7},{7,6},{8,9},{9,8},{10,11... | collective-permute-start | bytes 786440 | tf_op jit(solution)/shard_map/ppermute | solution.py:213
  30.4 30.1 %collective-permute-start.20 = (bf16[256,512]{1,0:T(8,128)(2,1)S(1)}, bf16[256,512]{1,0:T(8,128)(2,1)S(1)}, u32[]{:S(2)}, u32[]{:S(2)}) collective-permute-start(bf16[256,512]{1,0:T(8,128)(2,1)S(1)} %pad_maximum_fusion.refs_3_), channel_id=1, source_target_pairs={{0,16},{8,24},{16,0},{24,8},{1,17},{9,25},{17,1},{25,9},{2,18},{10... | collective-permute-start | bytes 786440 | tf_op jit(solution)/shard_map/ppermute | solution.py:211
  56.9 28.5 %collective-permute-start.10 = (bf16[256,512]{1,0:T(8,128)(2,1)S(1)}, bf16[256,512]{1,0:T(8,128)(2,1)S(1)}, u32[]{:S(2)}, u32[]{:S(2)}) collective-permute-start(bf16[256,512]{1,0:T(8,128)(2,1)S(1)} %get-tuple-element.16), channel_id=1, source_target_pairs={{0,17},{1,16},{2,19},{3,18},{4,21},{5,20},{6,23},{7,22},{8,25},{9,... | collective-permute-start | bytes 786440 | tf_op jit(solution)/shard_map/ppermute | solution.py:215
  57.8 27.6 %collective-permute-start.11 = (bf16[256,512]{1,0:T(8,128)(2,1)S(1)}, bf16[256,512]{1,0:T(8,128)(2,1)S(1)}, u32[]{:S(2)}, u32[]{:S(2)}) collective-permute-start(bf16[256,512]{1,0:T(8,128)(2,1)S(1)} %get-tuple-element.17), channel_id=1, source_target_pairs={{0,1},{1,0},{2,3},{3,2},{4,5},{5,4},{6,7},{7,6},{8,9},{9,8},{10,11... | collective-permute-start | bytes 786440 | tf_op jit(solution)/shard_map/ppermute | solution.py:213
  59.7 25.7 %collective-permute-start.12 = (bf16[256,512]{1,0:T(8,128)(2,1)S(1)}, bf16[256,512]{1,0:T(8,128)(2,1)S(1)}, u32[]{:S(2)}, u32[]{:S(2)}) collective-permute-start(bf16[256,512]{1,0:T(8,128)(2,1)S(1)} %get-tuple-element.18), channel_id=1, source_target_pairs={{0,16},{8,24},{16,0},{24,8},{1,17},{9,25},{17,1},{25,9},{2,18},{10... | collective-permute-start | bytes 786440 | tf_op jit(solution)/shard_map/ppermute | solution.py:211
  87.9 7.3 %collective-permute-start.22 = (bf16[128,512]{1,0:T(8,128)(2,1)S(1)}, bf16[128,512]{1,0:T(8,128)(2,1)S(1)}, u32[]{:S(2)}, u32[]{:S(2)}) collective-permute-start(bf16[128,512]{1,0:T(8,128)(2,1)S(1)} %get-tuple-element.29), channel_id=1, source_target_pairs={{0,17},{1,16},{2,19},{3,18},{4,21},{5,20},{6,23},{7,22},{8,25},{9,... | collective-permute-start | bytes 393224 | tf_op jit(solution)/shard_map/ppermute | solution.py:215
  88.7 8.2 %collective-permute-start.23 = (bf16[128,512]{1,0:T(8,128)(2,1)S(1)}, bf16[128,512]{1,0:T(8,128)(2,1)S(1)}, u32[]{:S(2)}, u32[]{:S(2)}) collective-permute-start(bf16[128,512]{1,0:T(8,128)(2,1)S(1)} %get-tuple-element.31), channel_id=1, source_target_pairs={{0,1},{1,0},{2,3},{3,2},{4,5},{5,4},{6,7},{7,6},{8,9},{9,8},{10,11... | collective-permute-start | bytes 393224 | tf_op jit(solution)/shard_map/ppermute | solution.py:213
  90.7 6.4 %collective-permute-start.24 = (bf16[128,512]{1,0:T(8,128)(2,1)S(1)}, bf16[128,512]{1,0:T(8,128)(2,1)S(1)}, u32[]{:S(2)}, u32[]{:S(2)}) collective-permute-start(bf16[128,512]{1,0:T(8,128)(2,1)S(1)} %get-tuple-element.30), channel_id=1, source_target_pairs={{0,16},{8,24},{16,0},{24,8},{1,17},{9,25},{17,1},{25,9},{2,18},{10... | collective-permute-start | bytes 393224 | tf_op jit(solution)/shard_map/ppermute | solution.py:211
  91.5 8.2 %collective-permute-start.14 = (bf16[128,128]{1,0:T(8,128)(2,1)S(1)}, bf16[128,128]{1,0:T(8,128)(2,1)S(1)}, u32[]{:S(2)}, u32[]{:S(2)}) collective-permute-start(bf16[128,128]{1,0:T(8,128)(2,1)S(1)} %get-tuple-element.32), channel_id=1, source_target_pairs={{0,6},{1,7},{2,4},{3,5},{4,2},{5,3},{6,0},{7,1},{8,14},{9,15},{10,... | collective-permute-start | bytes 98312 | tf_op jit(solution)/shard_map/ppermute | solution.py:221
  93.3 8.4 %collective-permute-start.15 = (bf16[128,128]{1,0:T(8,128)(2,1)S(1)}, bf16[128,128]{1,0:T(8,128)(2,1)S(1)}, u32[]{:S(2)}, u32[]{:S(2)}) collective-permute-start(bf16[128,128]{1,0:T(8,128)(2,1)S(1)} %get-tuple-element.34), channel_id=1, source_target_pairs={{0,4},{1,5},{2,6},{3,7},{4,0},{5,1},{6,2},{7,3},{8,12},{9,13},{10,... | collective-permute-start | bytes 98312 | tf_op jit(solution)/shard_map/ppermute | solution.py:221
  95.2 6.5 %collective-permute-start.16 = (bf16[128,128]{1,0:T(8,128)(2,1)S(1)}, bf16[128,128]{1,0:T(8,128)(2,1)S(1)}, u32[]{:S(2)}, u32[]{:S(2)}) collective-permute-start(bf16[128,128]{1,0:T(8,128)(2,1)S(1)} %get-tuple-element.33), channel_id=1, source_target_pairs={{0,2},{1,3},{2,0},{3,1},{4,6},{5,7},{6,4},{7,5},{8,10},{9,11},{10,... | collective-permute-start | bytes 98312 | tf_op jit(solution)/shard_map/ppermute | solution.py:221
  97.2 6.2 %collective-permute-start.25 = (bf16[128,128]{1,0:T(8,128)(2,1)S(1)}, bf16[128,128]{1,0:T(8,128)(2,1)S(1)}, u32[]{:S(2)}, u32[]{:S(2)}) collective-permute-start(bf16[128,128]{1,0:T(8,128)(2,1)S(1)} %get-tuple-element.35), channel_id=1, source_target_pairs={{0,6},{1,7},{2,4},{3,5},{4,2},{5,3},{6,0},{7,1},{8,14},{9,15},{10,... | collective-permute-start | bytes 98312 | tf_op jit(solution)/shard_map/ppermute | solution.py:221
  (7 other events, 19.8 us)
